TPU v7x, 256 devices: a whole 4x4x8 slice. The times are simulated.
256 devices in a mesh: roll: 32 (over z_lo, x, core), tp: 8 (over z_hi, y).
Axes of the slice: x: 4, y: 4, z: 8 (z_hi: 2, z_lo: 4; z = z_hi * 4 + z_lo), core: 2. Of those that a mesh axis runs over, the one named last changes fastest.
Arguments:
- prompt_states: bfloat16 [32, 1024, 2048], P('roll', 'tp'), may hold values from -6 to 6
- lengths: int32 [32], P('roll'), may hold values from 256 to 1024, as said below
- bucket_owner: int32 [32], replicated, may hold values from 0 to 31, each once
- w_in: bfloat16 [2048, 6, 2048], P('roll', None, 'tp'), may hold values from -0.125 to 0.125
- w_gates: bfloat16 [2048, 2, 2, 16], P('roll', None, None, 'tp'), may hold values from -0.125 to 0.125
- out_weight: bfloat16 [2048, 2, 2048], P('roll', None, 'tp'), may hold values from -0.09375 to 0.09375
- conv_weight: bfloat16 [4, 4, 2048], P(None, None, 'tp'), may hold values from -3 to 3
- decay_rate: float32 [2, 16], P(None, 'tp'), may hold values from 0.001 to 0.05
- dt_bias: float32 [2, 16], P(None, 'tp'), may hold values from -3 to 3
- in_gain: float32 [2048], replicated, may hold values from 0.5 to 1.5
- head_gain: float32 [128], replicated, may hold values from 0.5 to 1.5
Outputs:
- layer_out: bfloat16 [32, 1024, 2048], P('roll', 'tp')
Inputs may be any that keep to these rules, and one draw needn't show every extreme that they name: `lengths`: every prompt has at least 256 live positions, and some prompt has all 1024. `bucket_owner`: A permutation of the 32 row blocks.
All inputs are finite; a program needn't handle non-finite values.
Results may differ from a plain program's by a relative error of at most 0.015.
Values may be sent and summed in bfloat16 or wider, within the bound.
A program may use at most 64 MiB of HBM per device.

v0:
```python
import jax
import jax.numpy as jnp
from jax import lax
from jax.sharding import PartitionSpec as P

BLOCK = 64


HIGH = lax.Precision.HIGHEST


def delta_blocks(query, keys, values, decay, beta):
    heads_n, seq_len, depth = query.shape
    count = seq_len // BLOCK

    def split(array):
        return array.reshape((heads_n, count, BLOCK) + array.shape[2:]).swapaxes(0, 1)

    offsets = jnp.arange(BLOCK, dtype=jnp.int32)
    strict = offsets[:, None] > offsets[None, :]
    within = offsets[:, None] >= offsets[None, :]
    identity = jnp.eye(BLOCK, dtype=jnp.float32)

    def advance(state, blocks):
        block_q, block_k, block_v, block_g, block_b = blocks
        totals = jnp.cumsum(block_g, axis=-1)
        spans = totals[:, :, None] - totals[:, None, :]
        inside = jnp.where(within, jnp.exp(jnp.where(within, spans, 0.0)), 0.0)
        below = jnp.where(strict, inside, 0.0)
        key_key = jnp.einsum("hid,hjd->hij", block_k, block_k, precision=HIGH)
        system = identity + block_b[:, :, None] * key_key * below
        growth = jnp.exp(totals)
        right_side = jnp.concatenate(
            [block_b[..., None] * block_v, (block_b * growth)[..., None] * block_k], axis=-1
        )
        solved = lax.linalg.triangular_solve(
            system, right_side, left_side=True, lower=True, unit_diagonal=True
        )
        update = solved[..., :depth] - jnp.einsum(
            "hid,hde->hie", solved[..., depth:], state, precision=HIGH
        )
        scores = jnp.einsum("hid,hjd->hij", block_q, block_k, precision=HIGH) * inside
        outputs = growth[..., None] * jnp.einsum("hid,hde->hie", block_q, state, precision=HIGH)
        outputs = outputs + jnp.einsum("hij,hje->hie", scores, update, precision=HIGH)
        final_sum = totals[:, -1:]
        carry_weight = jnp.exp(final_sum - totals)
        new_state = jnp.exp(final_sum)[:, :, None] * state
        new_state = new_state + jnp.einsum(
            "hjd,hje->hde", block_k * carry_weight[..., None], update, precision=HIGH
        )
        return (new_state, outputs)

    start_state = jnp.zeros((heads_n, depth, depth), jnp.float32)
    _, outs = lax.scan(
        advance, start_state, (split(query), split(keys), split(values), split(decay), split(beta))
    )
    return outs.swapaxes(0, 1).reshape(heads_n, seq_len, depth)


def unit_rows(array):
    return array / jnp.sqrt(jnp.sum(array * array, axis=-1, keepdims=True) + 1e-06)


def causal_conv(parts, taps):
    seq_len = parts.shape[0]
    width = taps.shape[0]
    padded = jnp.pad(parts, ((width - 1, 0), (0, 0), (0, 0), (0, 0)))
    total = jnp.zeros(parts.shape, jnp.float32)
    for shift_by in range(width):
        begin = width - 1 - shift_by
        total = total + taps[shift_by] * padded[begin : begin + seq_len]
    return total


def mixer(projected, gate_logits, conv_weight, decay_rate, dt_bias, head_gain, heads, head_dim):
    seq_len = projected.shape[0]
    parts = projected.reshape(seq_len, 6, heads, head_dim)
    taps = conv_weight.astype(jnp.float32).reshape(conv_weight.shape[0], 4, heads, head_dim)
    mixed = jax.nn.silu(causal_conv(parts[:, :4], taps))
    query = unit_rows(mixed[:, 0]) * head_dim ** (-0.5)
    keys = unit_rows(mixed[:, 1])
    values = mixed[:, 2:4]
    gates = gate_logits.reshape(seq_len, 2, 2, heads)
    beta = jax.nn.sigmoid(gates[:, 1])
    decay = -decay_rate * jax.nn.softplus(gates[:, 0] + dt_bias)
    value_heads = 2 * heads
    values_h = values.transpose(1, 2, 0, 3).reshape(value_heads, seq_len, head_dim)
    query_h = jnp.broadcast_to(
        query.transpose(1, 0, 2)[None], (2, heads, seq_len, head_dim)
    ).reshape(value_heads, seq_len, head_dim)
    keys_h = jnp.broadcast_to(keys.transpose(1, 0, 2)[None], (2, heads, seq_len, head_dim)).reshape(
        value_heads, seq_len, head_dim
    )
    decay_h = decay.transpose(1, 2, 0).reshape(value_heads, seq_len)
    beta_h = beta.transpose(1, 2, 0).reshape(value_heads, seq_len)
    recur = delta_blocks(query_h, keys_h, values_h, decay_h, beta_h)
    recur = recur.reshape(2, heads, seq_len, head_dim).transpose(2, 0, 1, 3)
    normed = recur / jnp.sqrt(jnp.mean(recur * recur, axis=-1, keepdims=True) + 1e-06) * head_gain
    hidden = (normed * jax.nn.silu(parts[:, 4:6])).astype(jnp.bfloat16)
    return hidden.reshape(seq_len, 2 * heads * head_dim)


def norm_rows(rows, in_gain):
    return rows / jnp.sqrt(jnp.mean(rows * rows, axis=-1, keepdims=True) + 1e-06) * in_gain


def body(
    prompt_states,
    lengths,
    bucket_owner,
    w_in,
    w_gates,
    out_weight,
    conv_weight,
    decay_rate,
    dt_bias,
    in_gain,
    head_gain,
):
    tok_rows = prompt_states.shape[1]
    width = prompt_states.shape[2]
    own_rows = prompt_states[0]
    normed = norm_rows(own_rows.astype(jnp.float32), in_gain).astype(jnp.bfloat16)
    full_rows = lax.all_gather(normed, "tp", axis=0, tiled=True)
    seq_len = full_rows.shape[0]
    buckets = bucket_owner.shape[0]
    block_rows = width // buckets
    labels = jnp.arange(buckets, dtype=jnp.int32)
    matches = (bucket_owner[:, None] == labels[None, :]).astype(jnp.int32)
    inverse = jnp.sum(labels[:, None] * matches, axis=0)
    permuted = jnp.take(full_rows.reshape(seq_len, buckets, block_rows), inverse, axis=1).reshape(
        seq_len, width
    )
    local_heads = w_gates.shape[3]
    head_dim = head_gain.shape[0]
    all_in, all_gates, all_out = (
        lax.all_gather(w_in, "roll", axis=0, tiled=True),
        lax.all_gather(w_gates, "roll", axis=0, tiled=True),
        lax.all_gather(out_weight, "roll", axis=0, tiled=True),
    )
    projected = jnp.dot(permuted, all_in.reshape(width, -1), preferred_element_type=jnp.float32)
    gate_logits = jnp.dot(
        permuted, all_gates.reshape(width, -1), preferred_element_type=jnp.float32
    )
    hidden = mixer(
        projected, gate_logits, conv_weight, decay_rate, dt_bias, head_gain, local_heads, head_dim
    )
    out_matrix = all_out.reshape(width, -1)
    stored = lax.dot_general(
        hidden, out_matrix, (((1,), (1,)), ((), ())), preferred_element_type=jnp.float32
    )
    mine = lax.psum_scatter(
        jnp.take(
            stored.reshape(tok_rows * lax.axis_size("tp"), buckets, block_rows),
            bucket_owner,
            axis=1,
        )
        .reshape(tok_rows * lax.axis_size("tp"), width)
        .astype(jnp.bfloat16),
        "tp",
        scatter_dimension=0,
        tiled=True,
    ).astype(jnp.float32)
    positions = lax.axis_index("tp") * tok_rows + jnp.arange(tok_rows, dtype=jnp.int32)
    live = positions < lengths[0]
    result = jnp.where(live[:, None], mine, 0.0).astype(jnp.bfloat16)
    return result[None]


def solution(mesh):
    in_specs = (
        P("roll", "tp", None),
        P("roll"),
        P(),
        P("roll", None, "tp"),
        P("roll", None, None, "tp"),
        P("roll", None, "tp"),
        P(None, None, "tp"),
        P(None, "tp"),
        P(None, "tp"),
        P(),
        P(),
    )
    out_specs = P("roll", "tp", None)
    return jax.shard_map(body, mesh=mesh, in_specs=in_specs, out_specs=out_specs, check_vma=False)
```

profile of v0, /device:TPU:2, one launch (start us, length us, event | category | flops | bytes accessed | tf_op | source)
XLA Modules:
  0.0 869.4 jit_solution(16568466921655669896)
XLA Ops:
  12.4 48.9 %all_gather.13 = bf16[2048,2,2,2]{3,2,1,0:T(2,128)(2,1)S(1)} all-gather(bf16[64,2,2,2]{3,2,1,0:T(2,128)(2,1)S(1)} %copy.66), channel_id=1, replica_groups=mesh['roll'=32,'tp'=8] {'roll'}, dimensions={0}, use_global_device_ids=true | all-gather | bytes 33792 | tf_op jit(solution)/shard_map/all_gather | solution.py:138
  61.3 2.8 copy.67
  64.6 8.3 all-gather.8.cloned.1.call-done
  72.9 4.4 dot_general.43
  77.2 109.6 %all-gather.4.cloned.1.call-done = bf16[1024,2048]{0,1:T(8,128)(2,1)} async-done(((bf16[128,2048]{0,1:T(8,128)(2,1)}), bf16[1024,2048]{0,1:T(8,128)(2,1)}) %all-gather.4.cloned.1.call-update) | async-done | bytes 4194320 | tf_op jit(solution)/shard_map/all_gather | solution.py:124
  186.8 5.1 gather_fusion
  191.9 2.6 broadcast_select_fusion
  197.6 52.8 %all-gather.6.cloned.1.call-done = bf16[2048,6,256]{2,0,1:T(8,128)(2,1)} async-done(((bf16[64,6,256]{2,0,1:T(8,128)(2,1)}), bf16[2048,6,256]{2,0,1:T(8,128)(2,1)}) %all-gather.6.cloned.1.call-update) | async-done | bytes 6291472 | tf_op jit(solution)/shard_map/all_gather | solution.py:137
  250.4 8.6 copy.70
  259.1 10.3 %fusion.61 = f32[1024,6,2,128]{3,0,2,1:T(8,128)S(1)} fusion(bf16[1024,2048,1,1]{0,1,3,2:T(8,128)(2,1)} %bitcast.158, bf16[6,2,128,2048]{3,2,1,0:T(8,128)(2,1)} %bitcast.155), kind=kOutput, calls=%fused_computation.115 | convolution fusion | flops 6442450944 | bytes 16777216 | tf_op jit(solution)/shard_map/dot_general | solution.py:141
  269.4 2.6 copy-done
  272.3 2.6 divide_multiply_fusion
  279.5 426.7 %while.14 = (s32[]{:T(128)}, f32[4,128,128]{2,1,0:T(8,128)S(1)}, f32[16,4,64,128]{3,2,1,0:T(8,128)}, f32[16,4,64]{2,1,0:T(4,128)S(1)}, f32[16,4,64,128]{3,2,0,1:...) while((s32[]{:T(128)}, f32[4,128,128]{2,1,0:T(8,128)S(1)}, ...), condition=%wide.region_6.7_spmd.clone.clone, body=%wide.region_4.6_spmd.clone.clone.sunk | while | flops 277672256 | bytes 4235992 | solution.py:54
  282.8 19.7 %custom-call.12 = f32[4,1,64,64]{2,3,1,0:T(8,128)S(1)} custom-call(f32[4,1,64,64]{3,2,1,0:T(8,128)S(1)} %fusion.104), custom_call_target="InvertDiagBlocksLowerTriangular" | custom-call | tf_op jit(solution)/shard_map/while/body/eval_jaxpr/triangular_solve | solution.py:36
  303.6 1.9 fusion.107
  309.5 19.7 %custom-call.12 = f32[4,1,64,64]{2,3,1,0:T(8,128)S(1)} custom-call(f32[4,1,64,64]{3,2,1,0:T(8,128)S(1)} %fusion.104), custom_call_target="InvertDiagBlocksLowerTriangular" | custom-call | tf_op jit(solution)/shard_map/while/body/eval_jaxpr/triangular_solve | solution.py:36
  336.2 19.7 %custom-call.12 = f32[4,1,64,64]{2,3,1,0:T(8,128)S(1)} custom-call(f32[4,1,64,64]{3,2,1,0:T(8,128)S(1)} %fusion.104), custom_call_target="InvertDiagBlocksLowerTriangular" | custom-call | tf_op jit(solution)/shard_map/while/body/eval_jaxpr/triangular_solve | solution.py:36
  362.8 19.7 %custom-call.12 = f32[4,1,64,64]{2,3,1,0:T(8,128)S(1)} custom-call(f32[4,1,64,64]{3,2,1,0:T(8,128)S(1)} %fusion.104), custom_call_target="InvertDiagBlocksLowerTriangular" | custom-call | tf_op jit(solution)/shard_map/while/body/eval_jaxpr/triangular_solve | solution.py:36
  389.5 19.7 %custom-call.12 = f32[4,1,64,64]{2,3,1,0:T(8,128)S(1)} custom-call(f32[4,1,64,64]{3,2,1,0:T(8,128)S(1)} %fusion.104), custom_call_target="InvertDiagBlocksLowerTriangular" | custom-call | tf_op jit(solution)/shard_map/while/body/eval_jaxpr/triangular_solve | solution.py:36
  410.2 1.9 fusion.107
  416.2 19.7 %custom-call.12 = f32[4,1,64,64]{2,3,1,0:T(8,128)S(1)} custom-call(f32[4,1,64,64]{3,2,1,0:T(8,128)S(1)} %fusion.104), custom_call_target="InvertDiagBlocksLowerTriangular" | custom-call | tf_op jit(solution)/shard_map/while/body/eval_jaxpr/triangular_solve | solution.py:36
  436.9 1.9 fusion.107
  442.8 19.7 %custom-call.12 = f32[4,1,64,64]{2,3,1,0:T(8,128)S(1)} custom-call(f32[4,1,64,64]{3,2,1,0:T(8,128)S(1)} %fusion.104), custom_call_target="InvertDiagBlocksLowerTriangular" | custom-call | tf_op jit(solution)/shard_map/while/body/eval_jaxpr/triangular_solve | solution.py:36
  463.6 1.9 fusion.107
  469.5 19.7 %custom-call.12 = f32[4,1,64,64]{2,3,1,0:T(8,128)S(1)} custom-call(f32[4,1,64,64]{3,2,1,0:T(8,128)S(1)} %fusion.104), custom_call_target="InvertDiagBlocksLowerTriangular" | custom-call | tf_op jit(solution)/shard_map/while/body/eval_jaxpr/triangular_solve | solution.py:36
  490.2 1.9 fusion.107
  496.2 19.7 %custom-call.12 = f32[4,1,64,64]{2,3,1,0:T(8,128)S(1)} custom-call(f32[4,1,64,64]{3,2,1,0:T(8,128)S(1)} %fusion.104), custom_call_target="InvertDiagBlocksLowerTriangular" | custom-call | tf_op jit(solution)/shard_map/while/body/eval_jaxpr/triangular_solve | solution.py:36
  516.9 1.9 fusion.107
  522.8 19.7 %custom-call.12 = f32[4,1,64,64]{2,3,1,0:T(8,128)S(1)} custom-call(f32[4,1,64,64]{3,2,1,0:T(8,128)S(1)} %fusion.104), custom_call_target="InvertDiagBlocksLowerTriangular" | custom-call | tf_op jit(solution)/shard_map/while/body/eval_jaxpr/triangular_solve | solution.py:36
  543.6 1.9 fusion.107
  549.5 19.7 %custom-call.12 = f32[4,1,64,64]{2,3,1,0:T(8,128)S(1)} custom-call(f32[4,1,64,64]{3,2,1,0:T(8,128)S(1)} %fusion.104), custom_call_target="InvertDiagBlocksLowerTriangular" | custom-call | tf_op jit(solution)/shard_map/while/body/eval_jaxpr/triangular_solve | solution.py:36
  570.2 1.9 fusion.107
  576.2 19.7 %custom-call.12 = f32[4,1,64,64]{2,3,1,0:T(8,128)S(1)} custom-call(f32[4,1,64,64]{3,2,1,0:T(8,128)S(1)} %fusion.104), custom_call_target="InvertDiagBlocksLowerTriangular" | custom-call | tf_op jit(solution)/shard_map/while/body/eval_jaxpr/triangular_solve | solution.py:36
  602.8 19.7 %custom-call.12 = f32[4,1,64,64]{2,3,1,0:T(8,128)S(1)} custom-call(f32[4,1,64,64]{3,2,1,0:T(8,128)S(1)} %fusion.104), custom_call_target="InvertDiagBlocksLowerTriangular" | custom-call | tf_op jit(solution)/shard_map/while/body/eval_jaxpr/triangular_solve | solution.py:36
  623.6 1.9 fusion.107
  629.5 19.7 %custom-call.12 = f32[4,1,64,64]{2,3,1,0:T(8,128)S(1)} custom-call(f32[4,1,64,64]{3,2,1,0:T(8,128)S(1)} %fusion.104), custom_call_target="InvertDiagBlocksLowerTriangular" | custom-call | tf_op jit(solution)/shard_map/while/body/eval_jaxpr/triangular_solve | solution.py:36
  650.2 1.9 fusion.107
  656.2 19.7 %custom-call.12 = f32[4,1,64,64]{2,3,1,0:T(8,128)S(1)} custom-call(f32[4,1,64,64]{3,2,1,0:T(8,128)S(1)} %fusion.104), custom_call_target="InvertDiagBlocksLowerTriangular" | custom-call | tf_op jit(solution)/shard_map/while/body/eval_jaxpr/triangular_solve | solution.py:36
  676.9 1.9 fusion.107
  682.9 19.7 %custom-call.12 = f32[4,1,64,64]{2,3,1,0:T(8,128)S(1)} custom-call(f32[4,1,64,64]{3,2,1,0:T(8,128)S(1)} %fusion.104), custom_call_target="InvertDiagBlocksLowerTriangular" | custom-call | tf_op jit(solution)/shard_map/while/body/eval_jaxpr/triangular_solve | solution.py:36
  703.6 1.9 fusion.107
  708.6 2.3 multiply_convert_fusion
  712.3 5.5 fusion.62
  717.8 5.0 gather_fusion.1
  722.7 6.5 copy.79
  729.3 5.5 select_convert_fusion
  735.5 125.4 %reduce-scatter.2.cloned.1.call-done = bf16[128,2048]{1,0:T(8,128)(2,1)} async-done(((bf16[1024,2048]{1,0:T(8,128)(2,1)}), bf16[128,2048]{1,0:T(8,128)(2,1)}) %reduce-scatter.2.cloned.1.call-update) | async-done | bytes 524304 | tf_op jit(solution)/shard_map/reduce_scatter | solution.py:152
  860.9 2.0 fusion.48
  (310 shorter events, 105.4 us)
Async XLA Ops:
  6.5 57.6 %copy-start.5 = (f32[2,2]{1,0:T(2,128)S(1)}, f32[2,2]{1,0:T(2,128)}, u32[]{:S(2)}) copy-start(f32[2,2]{1,0:T(2,128)} %param.20) | copy-start | bytes 52
  6.5 57.6 %copy-start.3 = (bf16[4,4,256]{2,1,0:T(4,128)(2,1)S(1)}, bf16[4,4,256]{2,1,0:T(4,128)(2,1)}, u32[]{:S(2)}) copy-start(bf16[4,4,256]{2,1,0:T(4,128)(2,1)} %param.19) | copy-start | bytes 24580
  6.5 57.7 %copy-start.7 = (s32[32]{0:T(128)S(1)}, s32[32]{0:T(128)}, u32[]{:S(2)}) copy-start(s32[32]{0:T(128)} %param.15) | copy-start | bytes 388
  6.5 66.3 %all-gather.8.cloned.1.call-start = ((), (), s32[]{:S(2)}) async-start(), calls=%async_computation.3 | async-start | bytes 2162688 | tf_op jit(solution)/shard_map/all_gather | solution.py:139
  7.3 179.6 %all-gather.4.cloned.1.call-start = ((), (), s32[]{:S(2)}) async-start(), calls=%async_computation.1 | async-start | bytes 4718592 | tf_op jit(solution)/shard_map/all_gather | solution.py:124
  10.8 239.7 %all-gather.6.cloned.1.call-start = ((), (), s32[]{:S(2)}) async-start(), calls=%async_computation.2 | async-start | bytes 6488064 | tf_op jit(solution)/shard_map/all_gather | solution.py:137
  11.5 849.4 %reduce-scatter.2.cloned.1.call-start = ((), (), s32[]{:S(2)}) async-start(), calls=%async_computation.4 | async-start | bytes 4718592 | tf_op jit(solution)/shard_map/reduce_scatter | solution.py:152
  194.6 1.9 copy-start.1
  194.6 2.8 copy-start.4
  269.4 2.7 copy-start
  706.2 2.4 copy-start.6
  708.6 3.7 copy-start.2
Sparse Core Ops, SparseCore 0:
  9.2 63.5 all-gather.7
  75.3 111.4 all-gather.3
  188.7 61.6 all-gather.5
  734.9 125.9 reduce-scatter.1
where the time goes:
time: 871 us; the launch traced here: 869 us
  other arithmetic  357 us (41%)
  waiting for transfers between devices  298 us (34%)
  matrix products  101 us (12%)
  local copies, waits for them, and re-layouts  49.2 us (6%)
  blocking collectives  48.9 us (6%)
  between operations  14.1 us (2%)
    another operation x48, other arithmetic, advance(): lax.linalg.triangular_solve(system, right_side, left_side=True, lower=Tru...  316 us
    reduce_scatter x1, waiting for transfers between devices, body(): lax.psum_scatter(jnp.take(stored.reshape(tok_rows * lax.axis_size('tp'),...  125 us
    all_gather x1, waiting for transfers between devices, body(): full_rows = lax.all_gather(normed, 'tp', axis=0, tiled=True)  110 us
    all_gather x1, waiting for transfers between devices, body(): lax.all_gather(w_in, 'roll', axis=0, tiled=True)  52.8 us
    all_gather x1, blocking collectives, body(): lax.all_gather(w_gates, 'roll', axis=0, tiled=True)  48.9 us
    dot_general x16, matrix products, advance(): jnp.einsum('hid,hde->hie', block_q, state, precision=HIGH)  30.8 us
    dot_general x16, matrix products, advance(): jnp.einsum('hid,hjd->hij', block_q, block_k, precision=HIGH) * inside  20.1 us
  transfers between devices with their start and end apart: 4, of which 4 were waited for; matrix products, arithmetic and copies ran while one was open for 2% of the time, Pallas kernels for 0%

commit v1 on v0

v1 whole, which is shorter than its diff:
```python
import jax
import jax.numpy as jnp
from jax import lax
from jax.experimental import pallas as pl
from jax.experimental.pallas import tpu as pltpu
from jax.sharding import PartitionSpec as P

CH = 64
NG = 4
ROWS = CH * NG
F32 = jnp.float32
BF16 = jnp.bfloat16
HIGHEST = lax.Precision.HIGHEST


def mm(a, b):
    return jnp.dot(a, b, preferred_element_type=F32)


def mm_nt(a, b):
    return lax.dot_general(a, b, (((1,), (1,)), ((), ())), preferred_element_type=F32)


def mm_tn(a, b):
    return lax.dot_general(a, b, (((0,), (0,)), ((), ())), preferred_element_type=F32)


def mm_exact(a, b):
    return jnp.dot(a, b, preferred_element_type=F32, precision=HIGHEST)


def silu(v):
    return v / (1.0 + jnp.exp(-v))


def mixer_kernel(x_ref, w_ref, taps_ref, rate_ref, bias_ref, gain_ref, out_ref, pscr, oscr, state):
    step = pl.program_id(0)

    @pl.when(step == 0)
    def _():
        pscr[0:8, :] = jnp.zeros((8, 1024), F32)
        state[...] = jnp.zeros_like(state)

    @pl.when(step > 0)
    def _():
        pscr[0:8, :] = pscr[ROWS : ROWS + 8, :]

    x = x_ref[...]
    gates = mm(x, w_ref[:, 1536:1664])
    pscr[8 : 8 + ROWS, :] = mm(x, w_ref[:, 0:1024])

    biased = gates + bias_ref[...]
    soft = jnp.maximum(biased, 0.0) + jnp.log(1.0 + jnp.exp(-jnp.abs(biased)))
    decay = -rate_ref[...] * soft
    beta = 1.0 / (1.0 + jnp.exp(-gates))
    ri = lax.broadcasted_iota(jnp.int32, (ROWS, ROWS), 0)
    ci = lax.broadcasted_iota(jnp.int32, (ROWS, ROWS), 1)
    same = (ri // CH) == (ci // CH)
    tri = jnp.where(same & (ri >= ci), 1.0, 0.0)
    totals = mm_exact(tri, decay)
    lane_r = lax.broadcasted_iota(jnp.int32, (128, 256), 0)
    lane_c = lax.broadcasted_iota(jnp.int32, (128, 256), 1)
    spread = jnp.where(lane_r == lane_c // CH, 1.0, 0.0)
    spread_b = jnp.where(lane_r == lane_c // CH + 4, 1.0, 0.0)
    lane_r5 = lax.broadcasted_iota(jnp.int32, (128, 512), 0)
    lane_c5 = lax.broadcasted_iota(jnp.int32, (128, 512), 1)
    spread5 = jnp.where(lane_r5 == lane_c5 // 128, 1.0, 0.0)
    spread5_b = jnp.where(lane_r5 == lane_c5 // 128 + 4, 1.0, 0.0)
    tot_w = mm_exact(totals, spread)
    beta_w = mm_exact(beta, spread_b)
    tot_v = mm_exact(totals, spread5)
    beta_v = mm_exact(beta, spread5_b)
    grow_v = jnp.exp(tot_v)

    mixed = []
    for c in range(4):
        acc = None
        for i in range(4):
            term = taps_ref[i : i + 1, c * 256 : (c + 1) * 256] * pscr[8 - i : 8 - i + ROWS, c * 256 : (c + 1) * 256]
            acc = term if acc is None else acc + term
        mixed.append(silu(acc))

    def unit(v):
        parts = []
        for h in range(2):
            p = v[:, h * 128 : (h + 1) * 128]
            parts.append(p * lax.rsqrt(jnp.sum(p * p, axis=-1, keepdims=True) + 1e-6))
        return jnp.concatenate(parts, axis=1)

    query = (unit(mixed[0]) * (128.0 ** -0.5)).astype(BF16)
    keys_f = unit(mixed[1])
    keys = keys_f.astype(BF16)

    wi = lax.broadcasted_iota(jnp.int32, (CH, 256), 0)
    wj = lax.broadcasted_iota(jnp.int32, (CH, 256), 1) % CH
    eye = wi == wj
    lower = wi >= wj
    strict = wi > wj
    bd_mask = same
    kmask = (lax.broadcasted_iota(jnp.int32, (128, 256), 0) // CH) == (
        lax.broadcasted_iota(jnp.int32, (128, 256), 1) // 128
    )

    def bd(v):
        vb = v.astype(BF16)
        return jnp.where(bd_mask, jnp.concatenate([vb] * 4, axis=0), jnp.zeros((), BF16))

    chunks = range(NG)
    rows = [slice(c * CH, (c + 1) * CH) for c in chunks]
    sys_w, score_w = [], []
    for c in chunks:
        k_c, q_c = keys[rows[c]], query[rows[c]]
        k_bd = jnp.where(kmask, jnp.concatenate([k_c, k_c], axis=0), jnp.zeros((), BF16))
        both = mm_nt(jnp.concatenate([k_c, q_c], axis=0), k_bd)
        kk = jnp.concatenate([both[:CH], both[:CH]], axis=1)
        qk = jnp.concatenate([both[CH:], both[CH:]], axis=1)
        t_c = tot_w[rows[c]]
        t_row = jnp.sum(jnp.where(eye, t_c, 0.0), axis=0, keepdims=True)
        inside = jnp.where(lower, jnp.exp(jnp.where(lower, t_c - t_row, 0.0)), 0.0)
        sys_w.append(jnp.where(strict, beta_w[rows[c]] * kk * inside, 0.0))
        score_w.append(qk * inside)

    eye_f = jnp.where(eye, 1.0, 0.0)

    def block(n):
        return (wi // n) == (wj // n)

    base = [jnp.where(block(8), a, 0.0) for a in sys_w]
    base2 = [mm(d.astype(BF16), bd(d)) for d in base]
    base4 = [mm(d.astype(BF16), bd(d)) for d in base2]
    inv = [eye_f - d for d in base]
    inv = [t + mm(t.astype(BF16), bd(d)) for t, d in zip(inv, base2)]
    inv = [t + mm(t.astype(BF16), bd(d)) for t, d in zip(inv, base4)]
    for n in (16, 32, 64):
        pick = block(n) & jnp.logical_not(block(n // 2))
        low = [jnp.where(pick, a, 0.0).astype(BF16) for a in sys_w]
        mid = [mm(l, bd(t)) for l, t in zip(low, inv)]
        inv = [t - mm(t.astype(BF16), bd(m)) for t, m in zip(inv, mid)]
    fixed = []
    for c in chunks:
        a_hi = sys_w[c].astype(BF16)
        a_lo = (sys_w[c] - a_hi.astype(F32)).astype(BF16)
        t_hi = inv[c].astype(BF16)
        t_lo = (inv[c] - t_hi.astype(F32)).astype(BF16)
        both = mm(jnp.concatenate([a_hi, a_lo], axis=0), bd(t_hi))
        prod = both[:CH] + both[CH:] + mm(a_hi, bd(t_lo))
        resid = eye_f - inv[c] - prod
        fixed.append(inv[c] + mm(t_hi, bd(resid)))
    inv = fixed

    solved = []
    for c in chunks:
        parts = []
        for s in range(2):
            for h in range(2):
                n = s * 2 + h
                b = beta_v[rows[c], n * 128 : (n + 1) * 128]
                g = grow_v[rows[c], n * 128 : (n + 1) * 128]
                v = mixed[2 + s][rows[c], h * 128 : (h + 1) * 128]
                k = keys_f[rows[c], h * 128 : (h + 1) * 128]
                parts.append(jnp.concatenate([(b * v).astype(BF16), (b * g * k).astype(BF16)], axis=1))
        rhs = jnp.concatenate(parts, axis=0)
        solved.append(mm(bd(inv[c]), rhs))
    score_bd = [bd(s) for s in score_w]

    for c in chunks:
        reads = []
        for h in range(2):
            lhs = jnp.concatenate(
                [
                    solved[c][h * CH : (h + 1) * CH, 128:256].astype(BF16),
                    solved[c][(2 + h) * CH : (3 + h) * CH, 128:256].astype(BF16),
                    query[rows[c], h * 128 : (h + 1) * 128],
                ],
                axis=0,
            )
            reads.append(mm(lhs, state[h].astype(BF16)))
        updates, writes = [None] * 4, [None] * 4
        last = tot_v[(c + 1) * CH - 1 : (c + 1) * CH, :]
        for s in range(2):
            for h in range(2):
                n = s * 2 + h
                u = solved[c][n * CH : (n + 1) * CH, 0:128] - reads[h][s * CH : (s + 1) * CH, s * 128 : (s + 1) * 128]
                carry = jnp.exp(last[:, n * 128 : (n + 1) * 128] - tot_v[rows[c], n * 128 : (n + 1) * 128])
                updates[n] = u.astype(BF16)
                writes[n] = (carry * u).astype(BF16)
        for h in range(2):
            decay_all = jnp.concatenate(
                [jnp.exp(last[:, h * 128 : (h + 1) * 128]), jnp.exp(last[:, (2 + h) * 128 : (3 + h) * 128])], axis=1
            )
            write = jnp.concatenate([writes[h], writes[2 + h]], axis=1)
            state[h] = decay_all * state[h] + mm_tn(keys[rows[c], h * 128 : (h + 1) * 128], write)
        inner = mm(score_bd[c], jnp.concatenate(updates, axis=0))
        for s in range(2):
            for h in range(2):
                n = s * 2 + h
                oscr[rows[c], n * 128 : (n + 1) * 128] = (
                    grow_v[rows[c], n * 128 : (n + 1) * 128] * reads[h][2 * CH :, s * 128 : (s + 1) * 128]
                    + inner[n * CH : (n + 1) * CH]
                )

    og = mm(x, w_ref[:, 1024:1536])
    hidden = []
    for n in range(4):
        r = oscr[:, n * 128 : (n + 1) * 128]
        r = r * lax.rsqrt(jnp.mean(r * r, axis=-1, keepdims=True) + 1e-6) * gain_ref[...]
        hidden.append((r * silu(og[:, n * 128 : (n + 1) * 128])).astype(BF16))
    hidden = jnp.concatenate(hidden, axis=1)
    out_ref[...] = mm_nt(hidden, w_ref[:, 1664:2176]).astype(BF16)


def mixer(x, w, taps, rate, bias, gain):
    seq = x.shape[0]
    return pl.pallas_call(
        mixer_kernel,
        grid=(seq // ROWS,),
        out_shape=jax.ShapeDtypeStruct((seq, 2048), BF16),
        in_specs=[
            pl.BlockSpec((ROWS, 2048), lambda i: (i, 0)),
            pl.BlockSpec((2048, 2176), lambda i: (0, 0), pipeline_mode=pl.Buffered(1)),
            pl.BlockSpec((4, 1024), lambda i: (0, 0)),
            pl.BlockSpec((1, 128), lambda i: (0, 0)),
            pl.BlockSpec((1, 128), lambda i: (0, 0)),
            pl.BlockSpec((1, 128), lambda i: (0, 0)),
        ],
        out_specs=pl.BlockSpec((ROWS, 2048), lambda i: (i, 0)),
        scratch_shapes=[
            pltpu.VMEM((ROWS + 8, 1024), F32),
            pltpu.VMEM((ROWS, 512), F32),
            pltpu.VMEM((2, 128, 256), F32),
        ],
        compiler_params=pltpu.CompilerParams(vmem_limit_bytes=48 << 20),
        name="mixer",
    )(x, w, taps, rate, bias, gain)


def prep_kernel(owner_ref, x_ref, gain_ref, out_ref, scr, inverse):
    x = x_ref[...].astype(F32)
    scale = lax.rsqrt(jnp.mean(x * x, axis=-1, keepdims=True) + 1e-6)
    scr[...] = x * scale * gain_ref[...]
    for b in range(32):
        inverse[owner_ref[b]] = b
    low = lax.broadcasted_iota(jnp.int32, (128, 128), 1) < 64

    def half(block, side):
        tile = scr[:, pl.ds(pl.multiple_of((block // 2) * 128, 128), 128)]
        return jnp.where(block % 2 == side, tile, pltpu.roll(tile, 64, axis=1))

    for j in range(16):
        out_ref[:, j * 128 : (j + 1) * 128] = jnp.where(
            low, half(inverse[2 * j], 0), half(inverse[2 * j + 1], 1)
        ).astype(BF16)


def prep(owner, x, gain):
    return pl.pallas_call(
        prep_kernel,
        out_shape=jax.ShapeDtypeStruct(x.shape, BF16),
        in_specs=[
            pl.BlockSpec(memory_space=pltpu.SMEM),
            pl.BlockSpec(memory_space=pltpu.VMEM),
            pl.BlockSpec(memory_space=pltpu.VMEM),
        ],
        out_specs=pl.BlockSpec(memory_space=pltpu.VMEM),
        scratch_shapes=[pltpu.VMEM(x.shape, F32), pltpu.SMEM((32,), jnp.int32)],
        name="prep",
    )(owner, x, gain)


def finish_kernel(owner_ref, live_ref, x_ref, out_ref, scr):
    scr[...] = x_ref[...].astype(F32)
    live = lax.broadcasted_iota(jnp.int32, (128, 128), 0) < live_ref[0]
    low = lax.broadcasted_iota(jnp.int32, (128, 128), 1) < 64

    def half(block, side):
        tile = scr[:, pl.ds(pl.multiple_of((block // 2) * 128, 128), 128)]
        return jnp.where(block % 2 == side, tile, pltpu.roll(tile, 64, axis=1))

    for j in range(16):
        tile = jnp.where(low, half(owner_ref[2 * j], 0), half(owner_ref[2 * j + 1], 1))
        out_ref[:, j * 128 : (j + 1) * 128] = jnp.where(live, tile, 0.0).astype(BF16)


def finish(owner, live, x):
    return pl.pallas_call(
        finish_kernel,
        out_shape=jax.ShapeDtypeStruct(x.shape, BF16),
        in_specs=[
            pl.BlockSpec(memory_space=pltpu.SMEM),
            pl.BlockSpec(memory_space=pltpu.SMEM),
            pl.BlockSpec(memory_space=pltpu.VMEM),
        ],
        out_specs=pl.BlockSpec(memory_space=pltpu.VMEM),
        scratch_shapes=[pltpu.VMEM(x.shape, F32)],
        name="finish",
    )(owner, live, x)


def body(
    prompt_states,
    lengths,
    bucket_owner,
    w_in,
    w_gates,
    out_weight,
    conv_weight,
    decay_rate,
    dt_bias,
    in_gain,
    head_gain,
):
    tok_rows = prompt_states.shape[1]
    rows = w_in.shape[0]
    normed = prep(bucket_owner, prompt_states[0], in_gain[None, :])
    packed = jnp.concatenate(
        [
            w_in.reshape(rows, -1),
            jnp.pad(w_gates.reshape(rows, -1), ((0, 0), (0, 120))),
            out_weight.reshape(rows, -1),
        ],
        axis=1,
    )
    full_rows = lax.all_gather(normed, "tp", axis=0, tiled=True)
    weights = lax.all_gather(packed, "roll", axis=0, tiled=True)
    taps = conv_weight.astype(F32).reshape(4, -1)
    lane_pad = ((0, 0), (0, 124))
    rate = jnp.pad(decay_rate.reshape(1, -1), lane_pad)
    bias = jnp.pad(dt_bias.reshape(1, -1), lane_pad)
    partial = mixer(full_rows, weights, taps, rate, bias, head_gain[None, :])
    mine = lax.psum_scatter(partial, "tp", scatter_dimension=0, tiled=True)
    live = lengths - lax.axis_index("tp") * tok_rows
    return finish(bucket_owner, live, mine)[None]


def solution(mesh):
    in_specs = (
        P("roll", "tp", None),
        P("roll"),
        P(),
        P("roll", None, "tp"),
        P("roll", None, None, "tp"),
        P("roll", None, "tp"),
        P(None, None, "tp"),
        P(None, "tp"),
        P(None, "tp"),
        P(),
        P(),
    )
    out_specs = P("roll", "tp", None)
    return jax.shard_map(body, mesh=mesh, in_specs=in_specs, out_specs=out_specs, check_vma=False)
```

time: 871 us -> 363 us (0.42)
  other arithmetic: 357 us -> 1.45 us
  matrix products: 101 us -> 0 us
  blocking collectives: 48.9 us -> 0 us
  Pallas kernels: 0 us -> 43.8 us
  local copies, waits for them, and re-layouts: 49.2 us -> 6.69 us
    another operation x64 -> x0, other arithmetic: 320 us -> none  [the longest x48 316 us: advance(): lax.linalg.triangular_solve(system, right_side, left_side=True, lower=Tru...]
    dot_general x99 -> x0, matrix products: 93.8 us -> none  [the longest x16 30.8 us: advance(): jnp.einsum('hid,hde->hie', block_q, state, precision=HIGH)]
    all_gather x1 -> x0, blocking collectives: 48.9 us -> none  [body(): lax.all_gather(w_gates, 'roll', axis=0, tiled=True)]
    pallas_call x0 -> x3, Pallas kernels: none -> 43.8 us  [the longest x1 38.8 us: mixer(): pl.pallas_call(mixer_kernel, grid=(seq // ROWS,), out_shape=jax.ShapeDtyp...]
    mul x17 -> x0, other arithmetic: 19.3 us -> none  [the longest x16 16.7 us: advance(): (block_b * growth)[..., None] * block_k]
    gather x3 -> x0, local copies, waits for them, and re-layouts: 16.6 us -> none  [the longest x2 11.5 us: body(): jnp.take(stored.reshape(tok_rows * lax.axis_size('tp'), buckets, block_ro...]
    all_gather x2 -> x0, local copies, waits for them, and re-layouts: 11.4 us -> none  [the longest x1 8.63 us: body(): lax.all_gather(w_in, 'roll', axis=0, tiled=True)]
    convert_element_type x19 -> x0, other arithmetic: 9.73 us -> none  [the longest x1 5.49 us: body(): mine = lax.psum_scatter(jnp.take(stored.reshape(tok_rows * lax.axis_size(...]
  transfers between devices with their start and end apart: 4 -> 3, of which waited for: 4 -> 3; matrix products, arithmetic and copies ran while one was open for 2% -> 2% of each run, Pallas kernels for 0% -> 0%
where the time goes in v1:
time: 363 us
  waiting for transfers between devices  297 us (82%)
  Pallas kernels  43.8 us (12%)
  between operations  13.8 us (4%)
  local copies, waits for them, and re-layouts  6.69 us (2%)
    reduce_scatter x1, waiting for transfers between devices, body(): mine = lax.psum_scatter(partial, 'tp', scatter_dimension=0, tiled=True)  125 us
    all_gather x1, waiting for transfers between devices, body(): full_rows = lax.all_gather(normed, 'tp', axis=0, tiled=True)  105 us
    all_gather x1, waiting for transfers between devices, body(): weights = lax.all_gather(packed, 'roll', axis=0, tiled=True)  66.4 us
    pallas_call x1, Pallas kernels, mixer(): pl.pallas_call(mixer_kernel, grid=(seq // ROWS,), out_shape=jax.ShapeDtyp...  38.8 us
  transfers between devices with their start and end apart: 3, of which 3 were waited for; matrix products, arithmetic and copies ran while one was open for 2% of the time, Pallas kernels for 0%

profile of v1, /device:TPU:2, one launch (start us, length us, event | category | flops | bytes accessed | tf_op | source)
XLA Modules:
  0.0 362.6 jit_solution(3151859154896593875)
XLA Ops:
  6.5 0.0 all-gather.3.cloned.1.call-start
  6.5 2.6 prep.1
  9.1 0.0 all-gather.3.cloned.1.call-update
  9.2 0.0 all-gather.5.cloned.1.call-start
  9.2 0.9 copy.16
  10.1 0.9 copy.17
  11.0 0.8 copy.15
  11.8 0.8 fusion.3
  12.5 0.0 all-gather.5.cloned.1.call-update
  12.6 0.0 reduce-scatter.2.cloned.1.call-start
  12.6 0.7 convert_bitcast_fusion
  13.3 0.8 reshape.25
  14.1 0.8 reshape.26
  14.8 105.2 %all-gather.3.cloned.1.call-done.x_ref = bf16[1024,2048]{1,0:T(8,128)(2,1)} async-done(((bf16[128,2048]{1,0:T(8,128)(2,1)}), bf16[1024,2048]{1,0:T(8,128)(2,1)}) %all-gather.3.cloned.1.call-update) | async-done | bytes 4194320 | tf_op jit(solution)/shard_map/all_gather | solution.py:323
  120.0 66.4 %all-gather.5.cloned.1.call-done.w_ref = bf16[2048,2176]{1,0:T(8,128)(2,1)} async-done(((bf16[64,2176]{1,0:T(8,128)(2,1)}), bf16[2048,2176]{1,0:T(8,128)(2,1)}) %all-gather.5.cloned.1.call-update) | async-done | bytes 8912912 | tf_op jit(solution)/shard_map/all_gather | solution.py:324
  186.4 0.0 copy-start.1
  186.4 0.7 copy-done.1
  187.1 38.8 %mixer.1 = bf16[1024,2048]{1,0:T(8,128)(2,1)S(1)} custom-call(bf16[1024,2048]{1,0:T(8,128)(2,1)} %all-gather.3.cloned.1.call-done.x_ref, bf16[2048,2176]{1,0:T(8,128)(2,1)} %all-gather.5.cloned.1.call-done.w_ref, f32[4,1024]{1,0:T(4,128)S(1)} %bitcast.13, f32[1,128]{1,0:T(1,128)S(1)} %pad.12.rate_ref, f32[1,128]{1,0:T(1,128)S(1)} %pad.13.bias_ref, ...), custom_call_target="tpu_custom_call" | custom-call | tf_op jit(solution)/shard_map/mixer/pallas_call | solution.py:214
  225.9 0.0 copy-start
  225.9 1.9 copy-done
  227.8 0.0 reduce-scatter.2.cloned.1.call-update
  228.5 125.1 %reduce-scatter.2.cloned.1.call-done.x_ref = bf16[128,2048]{1,0:T(8,128)(2,1)} async-done(((bf16[1024,2048]{1,0:T(8,128)(2,1)}), bf16[128,2048]{1,0:T(8,128)(2,1)}) %reduce-scatter.2.cloned.1.call-update) | async-done | bytes 524304 | tf_op jit(solution)/shard_map/reduce_scatter | solution.py:330
  353.6 2.5 finish.1
  (3 shorter events, 0.0 us)
Async XLA Ops:
  6.5 113.5 %all-gather.3.cloned.1.call-start = ((), (), s32[]{:S(2)}) async-start(), calls=%async_computation.1 | async-start | bytes 4718592 | tf_op jit(solution)/shard_map/all_gather | solution.py:323
  9.2 177.3 %all-gather.5.cloned.1.call-start = ((), (), s32[]{:S(2)}) async-start(), calls=%async_computation.2 | async-start | bytes 9191424 | tf_op jit(solution)/shard_map/all_gather | solution.py:324
  12.6 341.1 %reduce-scatter.2.cloned.1.call-start = ((), (), s32[]{:S(2)}) async-start(), calls=%async_computation.3 | async-start | bytes 4718592 | tf_op jit(solution)/shard_map/reduce_scatter | solution.py:330
  186.4 0.7 copy-start.1
  225.9 1.9 copy-start
Sparse Core Ops, SparseCore 0:
  10.0 110.0 all-gather.2
  121.9 64.4 all-gather.4
  228.0 125.6 reduce-scatter.1

commit v2 on v1

--- a/solution.py
+++ b/solution.py
@@ -296,6 +296,313 @@
     )(owner, live, x)
 
 
+MESH = pl.DeviceIdType.MESH
+
+
+class Place:
+    def __init__(self):
+        roll, tp = lax.axis_index("roll"), lax.axis_index("tp")
+        self.zl, self.x, self.core = roll // 8, (roll // 2) % 4, roll % 2
+        self.zh, self.y = tp // 4, tp % 4
+
+    def at(self, zl=None, x=None, core=None, zh=None, y=None):
+        zl = self.zl if zl is None else zl
+        x = self.x if x is None else x
+        core = self.core if core is None else core
+        zh = self.zh if zh is None else zh
+        y = self.y if y is None else y
+        return (zl * 8 + x * 2 + core, zh * 4 + y)
+
+    def along_z(self, hops):
+        z = (self.zh * 4 + self.zl + hops) % 8
+        return self.at(zl=z % 4, zh=z // 4)
+
+
+def meet(devices):
+    barrier = pltpu.get_barrier_semaphore()
+    for device in devices:
+        pl.semaphore_signal(barrier, inc=1, device_id=device, device_id_type=MESH)
+    pl.semaphore_wait(barrier, len(devices))
+
+
+def gather_kernel(x_ref, w_ref, xo, wo, transit, zs_up, zs_dn, zr, ws, wr, ys, yr, own_sem):
+    me = Place()
+    left_x, right_x = me.at(x=(me.x + 3) % 4), me.at(x=(me.x + 1) % 4)
+    left_y, right_y = me.at(y=(me.y + 3) % 4), me.at(y=(me.y + 1) % 4)
+    up, down = me.at(zl=(me.zl + 1) % 4), me.at(zl=(me.zl + 3) % 4)
+    sibling, partner = me.at(core=1 - me.core), me.at(zh=1 - me.zh)
+    behind, ahead = me.along_z(6), me.along_z(2)
+    meet([left_x, right_x, left_y, right_y, up, down, sibling, partner, behind, ahead])
+
+    def copy(src, dst, send, recv, device):
+        return pltpu.make_async_remote_copy(
+            src_ref=src, dst_ref=dst, send_sem=send, recv_sem=recv, device_id=device, device_id_type=MESH
+        )
+
+    sent = []
+
+    def send(src, dst, sems, i, device):
+        c = copy(src, dst, sems[0].at[i], sems[1].at[i], device)
+        c.start()
+        sent.append(c)
+
+    def arrived(dst, sems, i):
+        copy(dst, dst, sems[0].at[i], sems[1].at[i], sibling).wait_recv()
+
+    W, Y = (ws, wr), (ys, yr)
+
+    def shard(zl, x, core):
+        return wo.at[pl.ds(pl.multiple_of((zl * 8 + x * 2 + core) * 64, 64), 64)]
+
+    def part(zl, x, core, p):
+        return wo.at[pl.ds(pl.multiple_of((zl * 8 + x * 2 + core) * 64 + p * 32, 32), 32)]
+
+    def block(zh, y, p):
+        return xo.at[pl.ds(pl.multiple_of((zh * 4 + y) * 128 + p * 64, 64), 64)]
+
+    order = [[0, 1, 2, 3], [1, 0, 2, 3], [2, 1, 3, 0], [3, 2, 1, 0]]
+    slot = [
+        jnp.where(me.zl == 0, order[0][j], jnp.where(me.zl == 1, order[1][j], jnp.where(me.zl == 2, order[2][j], order[3][j])))
+        for j in range(4)
+    ]
+    xl, xr = (me.x + 3) % 4, (me.x + 1) % 4
+    xf = (me.x + 2) % 4
+    yl, yr_, yf = (me.y + 3) % 4, (me.y + 1) % 4, (me.y + 2) % 4
+    mine_x = [x_ref.at[pl.ds(p * 64, 64)] for p in range(2)]
+
+    def z_up(src, z):
+        return copy(src, shard(z, me.x, me.core), zs_up.at[z], zr.at[z], up)
+
+    def z_down(src, z):
+        return copy(src, shard(z, me.x, me.core), zs_dn.at[z], zr.at[z], down)
+
+    def spread_x(src, j):
+        z = slot[j]
+        for i, device in ((0, right_x), (1, left_x)):
+            send(src, shard(z, me.x, me.core), W, j * 8 + i, device)
+        send(src, shard(z, me.x, me.core), W, j * 8 + 4, sibling)
+
+    def relay_x(j):
+        z = slot[j]
+        arrived(shard(z, xl, me.core), W, j * 8)
+        send(part(z, xl, me.core, 0), part(z, xl, me.core, 0), W, j * 8 + 2, right_x)
+        arrived(shard(z, xr, me.core), W, j * 8 + 1)
+        send(part(z, xr, me.core, 1), part(z, xr, me.core, 1), W, j * 8 + 3, left_x)
+        send(shard(z, xl, me.core), shard(z, xl, me.core), W, j * 8 + 5, sibling)
+        send(shard(z, xr, me.core), shard(z, xr, me.core), W, j * 8 + 6, sibling)
+
+    def far_x(j):
+        z = slot[j]
+        arrived(part(z, xf, me.core, 0), W, j * 8 + 2)
+        arrived(part(z, xf, me.core, 1), W, j * 8 + 3)
+        send(shard(z, xf, me.core), shard(z, xf, me.core), W, j * 8 + 7, sibling)
+
+    def take_z(j):
+        z = slot[j]
+        copy(shard(z, me.x, me.core), shard(z, me.x, me.core), zs_up.at[z], zr.at[z], up).wait_recv()
+
+        @pl.when((z < me.zl) & (me.zl < 3))
+        def _():
+            z_up(shard(z, me.x, me.core), z).start()
+
+        @pl.when((z > me.zl) & (me.zl > 0))
+        def _():
+            z_down(shard(z, me.x, me.core), z).start()
+
+        spread_x(shard(z, me.x, me.core), j)
+
+    def spread_y(src, zh, b, p):
+        send(src, block(zh, me.y, p), Y, b * 6 + p, right_y)
+        send(src, block(zh, me.y, p), Y, b * 6 + 2 + p, left_y)
+
+    def relay_y(zh, b):
+        arrived(block(zh, yl, 0), Y, b * 6)
+        send(block(zh, yl, 0), block(zh, yl, 0), Y, b * 6 + 4, right_y)
+        arrived(block(zh, yr_, 1), Y, b * 6 + 3)
+        send(block(zh, yr_, 1), block(zh, yr_, 1), Y, b * 6 + 5, left_y)
+
+    def rest_y(zh, b):
+        arrived(block(zh, yl, 1), Y, b * 6 + 1)
+        arrived(block(zh, yr_, 0), Y, b * 6 + 2)
+        arrived(block(zh, yf, 0), Y, b * 6 + 4)
+        arrived(block(zh, yf, 1), Y, b * 6 + 5)
+
+    other = 1 - me.zh
+    send(mine_x[1], transit, Y, 13, behind)
+    send(mine_x[0], block(me.zh, me.y, 0), Y, 12, partner)
+
+    @pl.when(me.zl < 3)
+    def _():
+        z_up(w_ref, me.zl).start()
+
+    @pl.when(me.zl > 0)
+    def _():
+        z_down(w_ref, me.zl).start()
+
+    spread_x(w_ref, 0)
+    spread_y(mine_x[0], me.zh, 0, 0)
+    spread_y(mine_x[1], me.zh, 0, 1)
+    keep_w = pltpu.make_async_copy(w_ref, shard(me.zl, me.x, me.core), own_sem.at[0])
+    keep_w.start()
+    keep_x = pltpu.make_async_copy(x_ref, xo.at[pl.ds(pl.multiple_of((me.zh * 4 + me.y) * 128, 128), 128)], own_sem.at[1])
+    keep_x.start()
+
+    relay_x(0)
+    take_z(1)
+    relay_y(me.zh, 0)
+    arrived(transit, Y, 13)
+    send(transit, block_of_ahead(me, xo), Y, 14, behind)
+    relay_x(1)
+    far_x(0)
+    take_z(2)
+    arrived(block(other, me.y, 0), Y, 12)
+    spread_y(block(other, me.y, 0), other, 1, 0)
+    relay_x(2)
+    far_x(1)
+    take_z(3)
+    arrived(block(other, me.y, 1), Y, 14)
+    spread_y(block(other, me.y, 1), other, 1, 1)
+    relay_x(3)
+    far_x(2)
+    relay_y(other, 1)
+    far_x(3)
+    rest_y(me.zh, 0)
+    rest_y(other, 1)
+    for j in range(4):
+        z = slot[j]
+        for i, x in ((4, me.x), (5, xl), (6, xr), (7, xf)):
+            arrived(shard(z, x, 1 - me.core), W, j * 8 + i)
+    keep_w.wait()
+    keep_x.wait()
+    for c in sent:
+        c.wait_send()
+    for j in range(4):
+        z = slot[j]
+
+        @pl.when((z <= me.zl) & (me.zl < 3))
+        def _():
+            z_up(shard(z, me.x, me.core), z).wait_send()
+
+        @pl.when((z >= me.zl) & (me.zl > 0))
+        def _():
+            z_down(shard(z, me.x, me.core), z).wait_send()
+
+
+def block_of_ahead(me, xo):
+    z = (me.zh * 4 + me.zl + 2) % 8
+    return xo.at[pl.ds(pl.multiple_of(((z // 4) * 4 + me.y) * 128 + 64, 64), 64)]
+
+
+DMA = pltpu.SemaphoreType.DMA
+
+
+def gather(rows, packed):
+    return pl.pallas_call(
+        gather_kernel,
+        out_shape=(
+            jax.ShapeDtypeStruct((8 * rows.shape[0], rows.shape[1]), BF16),
+            jax.ShapeDtypeStruct((32 * packed.shape[0], packed.shape[1]), BF16),
+        ),
+        in_specs=[pl.BlockSpec(memory_space=pl.ANY)] * 2,
+        out_specs=(pl.BlockSpec(memory_space=pl.ANY),) * 2,
+        scratch_shapes=[
+            pltpu.VMEM((64, 2048), BF16),
+            DMA((4,)), DMA((4,)), DMA((4,)),
+            DMA((32,)), DMA((32,)),
+            DMA((15,)), DMA((15,)),
+            DMA((2,)),
+        ],
+        compiler_params=pltpu.CompilerParams(collective_id=0, has_side_effects=True),
+        name="gather",
+    )(rows, packed)
+
+
+def scatter_kernel(p_ref, out_ref, first, full, mixed, summed, landed, transit, ss, rs):
+    me = Place()
+    left_y, right_y = me.at(y=(me.y + 3) % 4), me.at(y=(me.y + 1) % 4)
+    partner, behind, ahead = me.at(zh=1 - me.zh), me.along_z(6), me.along_z(2)
+    meet([left_y, right_y, partner, behind, ahead])
+    yl, yr_, yf = (me.y + 3) % 4, (me.y + 1) % 4, (me.y + 2) % 4
+    sent = []
+
+    def send(src, dst, i, device):
+        c = pltpu.make_async_remote_copy(
+            src_ref=src, dst_ref=dst, send_sem=ss.at[i], recv_sem=rs.at[i], device_id=device, device_id_type=MESH
+        )
+        c.start()
+        sent.append(c)
+
+    def arrived(dst, i):
+        pltpu.make_async_remote_copy(
+            src_ref=dst, dst_ref=dst, send_sem=ss.at[i], recv_sem=rs.at[i], device_id=partner, device_id_type=MESH
+        ).wait_recv()
+
+    def half(zh, y, p):
+        return p_ref.at[pl.ds(pl.multiple_of((zh * 4 + y) * 128 + p * 64, 64), 64)]
+
+    halves = (1 - me.zh, me.zh)
+    for b, zh in enumerate(halves):
+        send(half(zh, yf, 0), first.at[b, 0], b * 6, right_y)
+        send(half(zh, yf, 1), first.at[b, 1], b * 6 + 1, left_y)
+        send(half(zh, yr_, 1), full.at[b, 0, 1], b * 6 + 2, right_y)
+        send(half(zh, yl, 0), full.at[b, 1, 0], b * 6 + 3, left_y)
+
+    def relay(b, zh):
+        arrived(first.at[b, 0], b * 6)
+        mixed[b, 0] = (half(zh, yr_, 0)[...].astype(F32) + first[b, 0].astype(F32)).astype(BF16)
+        send(mixed.at[b, 0], full.at[b, 0, 0], b * 6 + 4, right_y)
+        arrived(first.at[b, 1], b * 6 + 1)
+        mixed[b, 1] = (half(zh, yl, 1)[...].astype(F32) + first[b, 1].astype(F32)).astype(BF16)
+        send(mixed.at[b, 1], full.at[b, 1, 1], b * 6 + 5, left_y)
+
+    def total(b, zh, p):
+        if p == 0:
+            arrived(full.at[b, 1, 0], b * 6 + 3)
+            arrived(full.at[b, 0, 0], b * 6 + 4)
+        else:
+            arrived(full.at[b, 0, 1], b * 6 + 2)
+            arrived(full.at[b, 1, 1], b * 6 + 5)
+        return half(zh, me.y, p)[...].astype(F32) + full[b, 0, p].astype(F32) + full[b, 1, p].astype(F32)
+
+    relay(0, halves[0])
+    summed[1] = total(0, halves[0], 1).astype(BF16)
+    send(summed.at[1], transit, 12, behind)
+    summed[0] = total(0, halves[0], 0).astype(BF16)
+    send(summed.at[0], landed.at[0], 13, partner)
+    relay(1, halves[1])
+    arrived(transit, 12)
+    send(transit, landed.at[1], 14, behind)
+    for p in range(2):
+        t = total(1, halves[1], p)
+        arrived(landed.at[p], 13 + p)
+        out_ref[p * 64 : (p + 1) * 64, :] = (t + landed[p].astype(F32)).astype(BF16)
+    for c in sent:
+        c.wait_send()
+
+
+def scatter(partial):
+    width = partial.shape[1]
+    return pl.pallas_call(
+        scatter_kernel,
+        out_shape=jax.ShapeDtypeStruct((partial.shape[0] // 8, width), BF16),
+        in_specs=[pl.BlockSpec(memory_space=pltpu.VMEM)],
+        out_specs=pl.BlockSpec(memory_space=pltpu.VMEM),
+        scratch_shapes=[
+            pltpu.VMEM((2, 2, 64, width), BF16),
+            pltpu.VMEM((2, 2, 2, 64, width), BF16),
+            pltpu.VMEM((2, 2, 64, width), BF16),
+            pltpu.VMEM((2, 64, width), BF16),
+            pltpu.VMEM((2, 64, width), BF16),
+            pltpu.VMEM((64, width), BF16),
+            DMA((15,)), DMA((15,)),
+        ],
+        compiler_params=pltpu.CompilerParams(
+            collective_id=1, has_side_effects=True, vmem_limit_bytes=32 << 20
+        ),
+        name="scatter",
+    )(partial)
+
+
 def body(
     prompt_states,
     lengths,
@@ -320,14 +627,13 @@
         ],
         axis=1,
     )
-    full_rows = lax.all_gather(normed, "tp", axis=0, tiled=True)
-    weights = lax.all_gather(packed, "roll", axis=0, tiled=True)
+    full_rows, weights = gather(normed, packed)
     taps = conv_weight.astype(F32).reshape(4, -1)
     lane_pad = ((0, 0), (0, 124))
     rate = jnp.pad(decay_rate.reshape(1, -1), lane_pad)
     bias = jnp.pad(dt_bias.reshape(1, -1), lane_pad)
     partial = mixer(full_rows, weights, taps, rate, bias, head_gain[None, :])
-    mine = lax.psum_scatter(partial, "tp", scatter_dimension=0, tiled=True)
+    mine = scatter(partial)
     live = lengths - lax.axis_index("tp") * tok_rows
     return finish(bucket_owner, live, mine)[None]
 

time: 363 us -> 195 us (0.54)
  waiting for transfers between devices: 297 us -> 0 us
  Pallas kernels: 43.8 us -> 187 us
  between operations: 13.8 us -> 0.7 us
    all_gather x2 -> x0, waiting for transfers between devices: 172 us -> none  [the longest x1 105 us: body(): full_rows = lax.all_gather(normed, 'tp', axis=0, tiled=True)]
    pallas_call x0 -> x2, Pallas kernels: none -> 143 us  [the longest x1 82.7 us: gather(): pl.pallas_call(gather_kernel, out_shape=(jax.ShapeDtypeStruct((8 * rows.s...]
    reduce_scatter x1 -> x0, waiting for transfers between devices: 125 us -> none  [body(): mine = lax.psum_scatter(partial, 'tp', scatter_dimension=0, tiled=True)]
  transfers between devices with their start and end apart: 3 -> 0, of which waited for: 3 -> 0; matrix products, arithmetic and copies ran while one was open for 2% -> 0% of each run, Pallas kernels for 0% -> 0%
where the time goes in v2:
time: 195 us; the launch traced here: 194 us
  Pallas kernels  187 us (96%)
  local copies, waits for them, and re-layouts  5.55 us (3%)
    pallas_call x1, Pallas kernels, gather(): pl.pallas_call(gather_kernel, out_shape=(jax.ShapeDtypeStruct((8 * rows.s...  82.7 us
    pallas_call x1, Pallas kernels, scatter(): pl.pallas_call(scatter_kernel, out_shape=jax.ShapeDtypeStruct((partial.sh...  59.9 us
    pallas_call x1, Pallas kernels, mixer(): pl.pallas_call(mixer_kernel, grid=(seq // ROWS,), out_shape=jax.ShapeDtyp...  38.8 us

profile of v2, /device:TPU:2, one launch (start us, length us, event | category | flops | bytes accessed | tf_op | source)
XLA Modules:
  0.0 194.2 jit_solution(10021610753781568422)
XLA Ops:
  0.0 0.9 copy.16
  0.9 0.9 copy.17
  1.8 0.8 copy.15
  2.6 0.8 fusion.3.w_ref
  3.3 2.6 %prep.1.x_ref = bf16[128,2048]{1,0:T(8,128)(2,1)} custom-call(s32[32]{0:T(128)} %owner_ref.3, bf16[128,2048]{1,0:T(8,128)(2,1)} %bitcast.16, f32[1,2048]{1,0:T(1,128)} %bitcast.20), custom_call_target="tpu_custom_call" | custom-call | tf_op jit(solution)/shard_map/prep/pallas_call | solution.py:256
  5.9 82.7 %gather.1 = (bf16[1024,2048]{1,0:T(8,128)(2,1)}, bf16[2048,2176]{1,0:T(8,128)(2,1)}) custom-call(bf16[128,2048]{1,0:T(8,128)(2,1)} %prep.1.x_ref, bf16[64,2176]{1,0:T(8,128)(2,1)} %fusion.3.w_ref), custom_call_target="tpu_custom_call" | custom-call | tf_op jit(solution)/shard_map/gather/pallas_call | solution.py:500
  88.7 0.7 convert_bitcast_fusion
  89.4 0.8 reshape.25
  90.1 0.8 reshape.26
  90.9 0.0 copy-start.1
  90.9 0.7 copy-done.1
  91.6 38.8 %mixer.1.p_ref = bf16[1024,2048]{1,0:T(8,128)(2,1)S(1)} custom-call(bf16[1024,2048]{1,0:T(8,128)(2,1)} %get-tuple-element.7.x_ref, bf16[2048,2176]{1,0:T(8,128)(2,1)} %get-tuple-element.8.w_ref, f32[4,1024]{1,0:T(4,128)S(1)} %bitcast.13, f32[1,128]{1,0:T(1,128)S(1)} %pad.12.rate_ref, f32[1,128]{1,0:T(1,128)S(1)} %pad.13.bias_ref, f32[1,128]{1,0:T(1,128)S(1)} %bitcast.14), custom_call_target="tpu_custom_call" | custom-call | tf_op jit(solution)/shard_map/mixer/pallas_call | solution.py:214
  130.3 59.9 %scatter.1.x_ref = bf16[128,2048]{1,0:T(8,128)(2,1)S(1)} custom-call(bf16[1024,2048]{1,0:T(8,128)(2,1)S(1)} %mixer.1.p_ref), custom_call_target="tpu_custom_call" | custom-call | tf_op jit(solution)/shard_map/scatter/pallas_call | solution.py:585
  190.3 0.0 copy-start
  190.3 0.8 copy-done
  191.7 2.5 %finish.1 = bf16[128,2048]{1,0:T(8,128)(2,1)} custom-call(s32[32]{0:T(128)} %owner_ref.3, s32[1]{0:T(128)S(6)} %sub.7.live_ref, bf16[128,2048]{1,0:T(8,128)(2,1)} %copy-done), custom_call_target="tpu_custom_call" | custom-call | tf_op jit(solution)/shard_map/finish/pallas_call | solution.py:285
  (3 shorter events, 0.0 us)
Async XLA Ops:
  90.9 0.7 copy-start.1
  190.3 0.8 copy-start

commit v3 on v1

--- a/solution.py
+++ b/solution.py
@@ -33,8 +33,424 @@
     return v / (1.0 + jnp.exp(-v))
 
 
-def mixer_kernel(x_ref, w_ref, taps_ref, rate_ref, bias_ref, gain_ref, out_ref, pscr, oscr, state):
+def prep_kernel(owner_ref, x_ref, gain_ref, out_ref, scr, inverse):
+    x = x_ref[...].astype(F32)
+    scale = lax.rsqrt(jnp.mean(x * x, axis=-1, keepdims=True) + 1e-6)
+    scr[...] = x * scale * gain_ref[...]
+    for b in range(32):
+        inverse[owner_ref[b]] = b
+    low = lax.broadcasted_iota(jnp.int32, (128, 128), 1) < 64
+
+    def half(block, side):
+        tile = scr[:, pl.ds(pl.multiple_of((block // 2) * 128, 128), 128)]
+        return jnp.where(block % 2 == side, tile, pltpu.roll(tile, 64, axis=1))
+
+    for j in range(16):
+        out_ref[:, j * 128 : (j + 1) * 128] = jnp.where(
+            low, half(inverse[2 * j], 0), half(inverse[2 * j + 1], 1)
+        ).astype(BF16)
+
+
+def prep(owner, x, gain):
+    return pl.pallas_call(
+        prep_kernel,
+        out_shape=jax.ShapeDtypeStruct(x.shape, BF16),
+        in_specs=[
+            pl.BlockSpec(memory_space=pltpu.SMEM),
+            pl.BlockSpec(memory_space=pltpu.VMEM),
+            pl.BlockSpec(memory_space=pltpu.VMEM),
+        ],
+        out_specs=pl.BlockSpec(memory_space=pltpu.VMEM),
+        scratch_shapes=[pltpu.VMEM(x.shape, F32), pltpu.SMEM((32,), jnp.int32)],
+        name="prep",
+    )(owner, x, gain)
+
+
+def finish_kernel(owner_ref, live_ref, x_ref, out_ref, scr):
+    scr[...] = x_ref[...].astype(F32)
+    live = lax.broadcasted_iota(jnp.int32, (128, 128), 0) < live_ref[0]
+    low = lax.broadcasted_iota(jnp.int32, (128, 128), 1) < 64
+
+    def half(block, side):
+        tile = scr[:, pl.ds(pl.multiple_of((block // 2) * 128, 128), 128)]
+        return jnp.where(block % 2 == side, tile, pltpu.roll(tile, 64, axis=1))
+
+    for j in range(16):
+        tile = jnp.where(low, half(owner_ref[2 * j], 0), half(owner_ref[2 * j + 1], 1))
+        out_ref[:, j * 128 : (j + 1) * 128] = jnp.where(live, tile, 0.0).astype(BF16)
+
+
+def finish(owner, live, x):
+    return pl.pallas_call(
+        finish_kernel,
+        out_shape=jax.ShapeDtypeStruct(x.shape, BF16),
+        in_specs=[
+            pl.BlockSpec(memory_space=pltpu.SMEM),
+            pl.BlockSpec(memory_space=pltpu.SMEM),
+            pl.BlockSpec(memory_space=pltpu.VMEM),
+        ],
+        out_specs=pl.BlockSpec(memory_space=pltpu.VMEM),
+        scratch_shapes=[pltpu.VMEM(x.shape, F32)],
+        name="finish",
+    )(owner, live, x)
+
+
+MESH = pl.DeviceIdType.MESH
+
+
+class Place:
+    def __init__(self):
+        roll, tp = lax.axis_index("roll"), lax.axis_index("tp")
+        self.zl, self.x, self.core = roll // 8, (roll // 2) % 4, roll % 2
+        self.zh, self.y = tp // 4, tp % 4
+
+    def at(self, zl=None, x=None, core=None, zh=None, y=None):
+        zl = self.zl if zl is None else zl
+        x = self.x if x is None else x
+        core = self.core if core is None else core
+        zh = self.zh if zh is None else zh
+        y = self.y if y is None else y
+        return (zl * 8 + x * 2 + core, zh * 4 + y)
+
+    def along_z(self, hops):
+        z = (self.zh * 4 + self.zl + hops) % 8
+        return self.at(zl=z % 4, zh=z // 4)
+
+
+def meet(devices):
+    barrier = pltpu.get_barrier_semaphore()
+    for device in devices:
+        pl.semaphore_signal(barrier, inc=1, device_id=device, device_id_type=MESH)
+    pl.semaphore_wait(barrier, len(devices))
+
+
+def gather_kernel(x_ref, w_ref, xo, wo, transit, zs_up, zs_dn, zr, ws, wr, ys, yr, own_sem):
+    me = Place()
+    left_x, right_x = me.at(x=(me.x + 3) % 4), me.at(x=(me.x + 1) % 4)
+    left_y, right_y = me.at(y=(me.y + 3) % 4), me.at(y=(me.y + 1) % 4)
+    up, down = me.at(zl=(me.zl + 1) % 4), me.at(zl=(me.zl + 3) % 4)
+    sibling, partner = me.at(core=1 - me.core), me.at(zh=1 - me.zh)
+    behind, ahead = me.along_z(6), me.along_z(2)
+    outer = (me.zh * 4 + me.zl + 2) % 8 < 4
+    meet([left_x, right_x, left_y, right_y, up, down, sibling, partner, behind, ahead])
+
+    def copy(src, dst, send, recv, device):
+        return pltpu.make_async_remote_copy(
+            src_ref=src, dst_ref=dst, send_sem=send, recv_sem=recv, device_id=device, device_id_type=MESH
+        )
+
+    sent = []
+
+    def send(src, dst, sems, i, device):
+        c = copy(src, dst, sems[0].at[i], sems[1].at[i], device)
+        c.start()
+        sent.append(c)
+
+    def arrived(dst, sems, i):
+        copy(dst, dst, sems[0].at[i], sems[1].at[i], sibling).wait_recv()
+
+    W, Y = (ws, wr), (ys, yr)
+
+    def shard(zl, x, core):
+        return wo.at[pl.ds(pl.multiple_of((zl * 8 + x * 2 + core) * 64, 64), 64)]
+
+    def part(zl, x, core, p):
+        return wo.at[pl.ds(pl.multiple_of((zl * 8 + x * 2 + core) * 64 + p * 32, 32), 32)]
+
+    def block(zh, y, p):
+        return xo.at[pl.ds(pl.multiple_of((zh * 4 + y) * 128 + p * 64, 64), 64)]
+
+    order = [[0, 1, 2, 3], [1, 2, 0, 3], [2, 1, 3, 0], [3, 2, 1, 0]]
+    slot = [
+        jnp.where(me.zl == 0, order[0][j], jnp.where(me.zl == 1, order[1][j], jnp.where(me.zl == 2, order[2][j], order[3][j])))
+        for j in range(4)
+    ]
+    xl, xr = (me.x + 3) % 4, (me.x + 1) % 4
+    xf = (me.x + 2) % 4
+    yl, yr_, yf = (me.y + 3) % 4, (me.y + 1) % 4, (me.y + 2) % 4
+    mine_x = [x_ref.at[pl.ds(p * 64, 64)] for p in range(2)]
+
+    def z_up(src, z):
+        return copy(src, shard(z, me.x, me.core), zs_up.at[z], zr.at[z], up)
+
+    def z_down(src, z):
+        return copy(src, shard(z, me.x, me.core), zs_dn.at[z], zr.at[z], down)
+
+    def spread_x(src, j):
+        z = slot[j]
+        for i, device in ((0, right_x), (1, left_x)):
+            send(src, shard(z, me.x, me.core), W, j * 8 + i, device)
+        send(src, shard(z, me.x, me.core), W, j * 8 + 4, sibling)
+
+    def relay_x(j):
+        z = slot[j]
+        arrived(shard(z, xl, me.core), W, j * 8)
+        send(part(z, xl, me.core, 0), part(z, xl, me.core, 0), W, j * 8 + 2, right_x)
+        arrived(shard(z, xr, me.core), W, j * 8 + 1)
+        send(part(z, xr, me.core, 1), part(z, xr, me.core, 1), W, j * 8 + 3, left_x)
+        send(shard(z, xl, me.core), shard(z, xl, me.core), W, j * 8 + 5, sibling)
+        send(shard(z, xr, me.core), shard(z, xr, me.core), W, j * 8 + 6, sibling)
+
+    def far_x(j):
+        z = slot[j]
+        arrived(part(z, xf, me.core, 0), W, j * 8 + 2)
+        arrived(part(z, xf, me.core, 1), W, j * 8 + 3)
+        send(shard(z, xf, me.core), shard(z, xf, me.core), W, j * 8 + 7, sibling)
+
+    def take_z(j):
+        z = slot[j]
+        copy(shard(z, me.x, me.core), shard(z, me.x, me.core), zs_up.at[z], zr.at[z], up).wait_recv()
+
+        @pl.when((z < me.zl) & (me.zl < 3))
+        def _():
+            z_up(shard(z, me.x, me.core), z).start()
+
+        @pl.when((z > me.zl) & (me.zl > 0))
+        def _():
+            z_down(shard(z, me.x, me.core), z).start()
+
+        spread_x(shard(z, me.x, me.core), j)
+
+    def spread_y(src, zh, b, p):
+        send(src, block(zh, me.y, p), Y, b * 6 + p, right_y)
+        send(src, block(zh, me.y, p), Y, b * 6 + 2 + p, left_y)
+
+    def relay_y(zh, b):
+        arrived(block(zh, yl, 0), Y, b * 6)
+        send(block(zh, yl, 0), block(zh, yl, 0), Y, b * 6 + 4, right_y)
+        arrived(block(zh, yr_, 1), Y, b * 6 + 3)
+        send(block(zh, yr_, 1), block(zh, yr_, 1), Y, b * 6 + 5, left_y)
+
+    def rest_y(zh, b):
+        arrived(block(zh, yl, 1), Y, b * 6 + 1)
+        arrived(block(zh, yr_, 0), Y, b * 6 + 2)
+        arrived(block(zh, yf, 0), Y, b * 6 + 4)
+        arrived(block(zh, yf, 1), Y, b * 6 + 5)
+
+    other = 1 - me.zh
+
+    def away():
+        i = 13 + 2 * me.zh
+        return copy(mine_x[1], transit.at[me.zh], ys.at[i], yr.at[i], me.along_z(jnp.where(me.zh == 0, 6, 2)))
+
+    def onward(s):
+        i = 14 + 2 * s
+        return copy(transit.at[s], block(s, me.y, 1), ys.at[i], yr.at[i], ahead if s else behind)
+
+
+    @pl.when(me.zl < 3)
+    def _():
+        z_up(w_ref, me.zl).start()
+
+    @pl.when(me.zl > 0)
+    def _():
+        z_down(w_ref, me.zl).start()
+
+    spread_x(w_ref, 0)
+    away().start()
+    send(mine_x[0], block(me.zh, me.y, 0), Y, 12, partner)
+    spread_y(mine_x[0], me.zh, 0, 0)
+    spread_y(mine_x[1], me.zh, 0, 1)
+    keep_w = pltpu.make_async_copy(w_ref, shard(me.zl, me.x, me.core), own_sem.at[0])
+    keep_w.start()
+    keep_x = pltpu.make_async_copy(x_ref, xo.at[pl.ds(pl.multiple_of((me.zh * 4 + me.y) * 128, 128), 128)], own_sem.at[1])
+    keep_x.start()
+
+    take_z(1)
+    relay_x(0)
+    take_z(2)
+    relay_y(me.zh, 0)
+
+    @pl.when(outer)
+    def _():
+        for s in range(2):
+            arrived(transit.at[s], Y, 13 + 2 * s)
+            onward(s).start()
+
+    relay_x(1)
+    take_z(3)
+    far_x(0)
+    relay_x(2)
+    arrived(block(other, me.y, 0), Y, 12)
+    spread_y(block(other, me.y, 0), other, 1, 0)
+    far_x(1)
+    arrived(block(other, me.y, 1), Y, 14 + 2 * other)
+    spread_y(block(other, me.y, 1), other, 1, 1)
+    relay_x(3)
+    far_x(2)
+    relay_y(other, 1)
+    far_x(3)
+    rest_y(me.zh, 0)
+    rest_y(other, 1)
+    for j in range(4):
+        z = slot[j]
+        for i, x in ((4, me.x), (5, xl), (6, xr), (7, xf)):
+            arrived(shard(z, x, 1 - me.core), W, j * 8 + i)
+    keep_w.wait()
+    keep_x.wait()
+    for c in sent:
+        c.wait_send()
+    away().wait_send()
+
+    @pl.when(outer)
+    def _():
+        for s in range(2):
+            onward(s).wait_send()
+
+    for j in range(4):
+        z = slot[j]
+
+        @pl.when((z <= me.zl) & (me.zl < 3))
+        def _():
+            z_up(shard(z, me.x, me.core), z).wait_send()
+
+        @pl.when((z >= me.zl) & (me.zl > 0))
+        def _():
+            z_down(shard(z, me.x, me.core), z).wait_send()
+
+
+DMA = pltpu.SemaphoreType.DMA
+
+
+def gather(rows, packed):
+    return pl.pallas_call(
+        gather_kernel,
+        out_shape=(
+            jax.ShapeDtypeStruct((8 * rows.shape[0], rows.shape[1]), BF16),
+            jax.ShapeDtypeStruct((32 * packed.shape[0], packed.shape[1]), BF16),
+        ),
+        in_specs=[pl.BlockSpec(memory_space=pl.ANY)] * 2,
+        out_specs=(pl.BlockSpec(memory_space=pl.ANY),) * 2,
+        scratch_shapes=[
+            pltpu.VMEM((2, 64, 2048), BF16),
+            DMA((4,)), DMA((4,)), DMA((4,)),
+            DMA((32,)), DMA((32,)),
+            DMA((17,)), DMA((17,)),
+            DMA((2,)),
+        ],
+        compiler_params=pltpu.CompilerParams(collective_id=0, has_side_effects=True),
+        name="gather",
+    )(rows, packed)
+
+
+class Sums:
+    def __init__(self, p_ref, first, full, mixed, kept, summed, landed, transit, ss, rs):
+        self.p, self.first, self.full, self.mixed = p_ref, first, full, mixed
+        self.kept, self.summed, self.landed, self.transit = kept, summed, landed, transit
+        self.ss, self.rs = ss, rs
+        me = self.me = Place()
+        self.left, self.right = me.at(y=(me.y + 3) % 4), me.at(y=(me.y + 1) % 4)
+        self.partner, self.behind, self.ahead = me.at(zh=1 - me.zh), me.along_z(6), me.along_z(2)
+        self.outer = (me.zh * 4 + me.zl + 2) % 8 < 4
+
+    def meet(self):
+        meet([self.left, self.right, self.partner, self.behind, self.ahead])
+
+    def copy(self, i, src, dst, device):
+        return pltpu.make_async_remote_copy(
+            src_ref=src, dst_ref=dst, send_sem=self.ss.at[i], recv_sem=self.rs.at[i], device_id=device, device_id_type=MESH
+        )
+
+    def half(self, b, y, p):
+        return self.p.at[pl.ds(pl.multiple_of((b * 4 + y) * 128 + p * 64, 64), 64)]
+
+    def message(self, b, k):
+        y, first, full = self.me.y, self.first, self.full
+        far, right, left = (y + 2) % 4, (y + 1) % 4, (y + 3) % 4
+        src, dst = (
+            (self.half(b, far, 0), first.at[b, 0]),
+            (self.half(b, far, 1), first.at[b, 1]),
+            (self.half(b, right, 1), full.at[b, 0, 1]),
+            (self.half(b, left, 0), full.at[b, 1, 0]),
+            (self.mixed.at[b, 0], full.at[b, 0, 0]),
+            (self.mixed.at[b, 1], full.at[b, 1, 1]),
+        )[k]
+        return self.copy(b * 6 + k, src, dst, self.left if k % 2 else self.right)
+
+    def begin(self, b):
+        for k in range(4):
+            self.message(b, k).start()
+
+    def relay(self, b):
+        y = self.me.y
+        for p, near in ((0, (y + 1) % 4), (1, (y + 3) % 4)):
+            self.message(b, p).wait_recv()
+            self.mixed[b, p] = (self.half(b, near, p)[...].astype(F32) + self.first[b, p].astype(F32)).astype(BF16)
+            self.message(b, 4 + p).start()
+
+    def across(self, b, p):
+        if p == 0:
+            return self.copy(12, self.summed.at[0], self.landed.at[0], self.partner)
+        return self.copy(13 + 2 * b, self.summed.at[1], self.transit.at[b], self.behind if b else self.ahead)
+
+    def passing(self, b):
+        return self.copy(14 + 2 * b, self.transit.at[b], self.landed.at[1], self.behind if b else self.ahead)
+
+    def total(self, b):
+        for p in (1, 0):
+            for k in ((3, 4), (2, 5))[p]:
+                self.message(b, k).wait_recv()
+            value = (
+                self.half(b, self.me.y, p)[...].astype(F32)
+                + self.full[b, 0, p].astype(F32)
+                + self.full[b, 1, p].astype(F32)
+            )
+
+            @pl.when(self.me.zh == b)
+            def _():
+                self.kept[p] = value
+
+            @pl.when(self.me.zh != b)
+            def _():
+                self.summed[p] = value.astype(BF16)
+                self.across(b, p).start()
+
+    def pass_on(self, b):
+        @pl.when(self.outer)
+        def _():
+            self.across(b, 1).wait_recv()
+            self.passing(b).start()
+
+    def finish(self, out_ref):
+        self.across(0, 0).wait_recv()
+        for b in range(2):
+
+            @pl.when(self.me.zh == b)
+            def _():
+                self.passing(b).wait_recv()
+
+        for p in range(2):
+            out_ref[p * 64 : (p + 1) * 64, :] = (self.kept[p] + self.landed[p].astype(F32)).astype(BF16)
+        for b in range(2):
+            for k in range(6):
+                self.message(b, k).wait_send()
+        self.across(0, 0).wait_send()
+        for b in range(2):
+
+            @pl.when(self.me.zh != b)
+            def _():
+                self.across(b, 1).wait_send()
+
+            @pl.when(self.outer)
+            def _():
+                self.passing(b).wait_send()
+
+
+def mixer_kernel(
+    x_ref, w_ref, taps_ref, rate_ref, bias_ref, gain_ref, out_ref,
+    pscr, oscr, state, p_ref, first, full, mixed, kept, summed, landed, transit, ss, rs,
+):
     step = pl.program_id(0)
+    across = Sums(p_ref, first, full, mixed, kept, summed, landed, transit, ss, rs)
+
+    @pl.when(step == 0)
+    def _():
+        across.meet()
+
+    @pl.when(step == 2)
+    def _():
+        across.begin(0)
+
 
     @pl.when(step == 0)
     def _():
@@ -49,34 +465,47 @@
     gates = mm(x, w_ref[:, 1536:1664])
     pscr[8 : 8 + ROWS, :] = mm(x, w_ref[:, 0:1024])
 
-    biased = gates + bias_ref[...]
+    lane = lax.broadcasted_iota(jnp.int32, (1, 128), 1)
+    rate, bias = jnp.zeros((1, 128), F32), jnp.zeros((1, 128), F32)
+    for n in range(4):
+        rate = jnp.where(lane == n, rate_ref[n // 2, n % 2], rate)
+        bias = jnp.where(lane == n, bias_ref[n // 2, n % 2], bias)
+    biased = gates + bias
     soft = jnp.maximum(biased, 0.0) + jnp.log(1.0 + jnp.exp(-jnp.abs(biased)))
-    decay = -rate_ref[...] * soft
     beta = 1.0 / (1.0 + jnp.exp(-gates))
+    is_decay, is_beta = lane < 4, (lane >= 4) & (lane < 8)
     ri = lax.broadcasted_iota(jnp.int32, (ROWS, ROWS), 0)
     ci = lax.broadcasted_iota(jnp.int32, (ROWS, ROWS), 1)
     same = (ri // CH) == (ci // CH)
-    tri = jnp.where(same & (ri >= ci), 1.0, 0.0)
-    totals = mm_exact(tri, decay)
-    lane_r = lax.broadcasted_iota(jnp.int32, (128, 256), 0)
-    lane_c = lax.broadcasted_iota(jnp.int32, (128, 256), 1)
-    spread = jnp.where(lane_r == lane_c // CH, 1.0, 0.0)
-    spread_b = jnp.where(lane_r == lane_c // CH + 4, 1.0, 0.0)
-    lane_r5 = lax.broadcasted_iota(jnp.int32, (128, 512), 0)
-    lane_c5 = lax.broadcasted_iota(jnp.int32, (128, 512), 1)
-    spread5 = jnp.where(lane_r5 == lane_c5 // 128, 1.0, 0.0)
-    spread5_b = jnp.where(lane_r5 == lane_c5 // 128 + 4, 1.0, 0.0)
-    tot_w = mm_exact(totals, spread)
-    beta_w = mm_exact(beta, spread_b)
-    tot_v = mm_exact(totals, spread5)
-    beta_v = mm_exact(beta, spread5_b)
+    tri = jnp.where(same & (ri >= ci), 1.0, 0.0).astype(BF16)
+
+    def thirds(v):
+        hi = v.astype(BF16).astype(F32)
+        rest = v - hi
+        mid = rest.astype(BF16).astype(F32)
+        return (hi + pltpu.roll(mid, 8, axis=1) + pltpu.roll(rest - mid, 16, axis=1)).astype(BF16)
+
+    sums = mm(tri, thirds(jnp.where(is_decay, -rate * soft, 0.0)))
+    sums = sums + pltpu.roll(sums, 120, axis=1) + pltpu.roll(sums, 112, axis=1)
+    both = thirds(jnp.where(is_decay, sums, jnp.where(is_beta, beta, 0.0)))
+
+    def spread(first, width):
+        r = lax.broadcasted_iota(jnp.int32, (128, 4 * width), 0)
+        c = lax.broadcasted_iota(jnp.int32, (128, 4 * width), 1)
+        return jnp.where((r < 24) & (r % 8 == c // width + first), 1.0, 0.0).astype(BF16)
+
+    tot_w = mm(both, spread(0, CH))
+    beta_w = mm(both, spread(4, CH))
+    tot_v = mm(both, spread(0, 128))
+    beta_v = mm(both, spread(4, 128))
     grow_v = jnp.exp(tot_v)
 
     mixed = []
+    taps = [taps_ref[i].astype(F32) for i in range(4)]
     for c in range(4):
         acc = None
         for i in range(4):
-            term = taps_ref[i : i + 1, c * 256 : (c + 1) * 256] * pscr[8 - i : 8 - i + ROWS, c * 256 : (c + 1) * 256]
+            term = taps[i][c : c + 1] * pscr[8 - i : 8 - i + ROWS, c * 256 : (c + 1) * 256]
             acc = term if acc is None else acc + term
         mixed.append(silu(acc))
 
@@ -206,94 +635,56 @@
         r = r * lax.rsqrt(jnp.mean(r * r, axis=-1, keepdims=True) + 1e-6) * gain_ref[...]
         hidden.append((r * silu(og[:, n * 128 : (n + 1) * 128])).astype(BF16))
     hidden = jnp.concatenate(hidden, axis=1)
-    out_ref[...] = mm_nt(hidden, w_ref[:, 1664:2176]).astype(BF16)
+    p_ref[pl.ds(pl.multiple_of(step * ROWS, ROWS), ROWS), :] = mm_nt(hidden, w_ref[:, 1664:2176]).astype(BF16)
+
+    @pl.when(step == 2)
+    def _():
+        across.relay(0)
+
+    @pl.when(step == 3)
+    def _():
+        across.begin(1)
+        across.total(0)
+        across.relay(1)
+        across.pass_on(0)
+        across.total(1)
+        across.pass_on(1)
+        across.finish(out_ref)
 
 
 def mixer(x, w, taps, rate, bias, gain):
-    seq = x.shape[0]
+    seq, width = x.shape
+    whole = lambda i: (0, 0)
     return pl.pallas_call(
         mixer_kernel,
         grid=(seq // ROWS,),
-        out_shape=jax.ShapeDtypeStruct((seq, 2048), BF16),
+        out_shape=jax.ShapeDtypeStruct((seq // 8, width), BF16),
         in_specs=[
             pl.BlockSpec((ROWS, 2048), lambda i: (i, 0)),
-            pl.BlockSpec((2048, 2176), lambda i: (0, 0), pipeline_mode=pl.Buffered(1)),
-            pl.BlockSpec((4, 1024), lambda i: (0, 0)),
-            pl.BlockSpec((1, 128), lambda i: (0, 0)),
-            pl.BlockSpec((1, 128), lambda i: (0, 0)),
-            pl.BlockSpec((1, 128), lambda i: (0, 0)),
+            pl.BlockSpec((2048, 2176), whole, pipeline_mode=pl.Buffered(1)),
+            pl.BlockSpec((4, 4, 256), lambda i: (0, 0, 0)),
+            pl.BlockSpec(memory_space=pltpu.SMEM),
+            pl.BlockSpec(memory_space=pltpu.SMEM),
+            pl.BlockSpec((1, 128), whole),
         ],
-        out_specs=pl.BlockSpec((ROWS, 2048), lambda i: (i, 0)),
+        out_specs=pl.BlockSpec((seq // 8, width), whole),
         scratch_shapes=[
             pltpu.VMEM((ROWS + 8, 1024), F32),
             pltpu.VMEM((ROWS, 512), F32),
             pltpu.VMEM((2, 128, 256), F32),
+            pltpu.VMEM((seq, width), BF16),
+            pltpu.VMEM((2, 2, 64, width), BF16),
+            pltpu.VMEM((2, 2, 2, 64, width), BF16),
+            pltpu.VMEM((2, 2, 64, width), BF16),
+            pltpu.VMEM((2, 64, width), F32),
+            pltpu.VMEM((2, 64, width), BF16),
+            pltpu.VMEM((2, 64, width), BF16),
+            pltpu.VMEM((2, 64, width), BF16),
+            DMA((17,)), DMA((17,)),
         ],
-        compiler_params=pltpu.CompilerParams(vmem_limit_bytes=48 << 20),
+        compiler_params=pltpu.CompilerParams(collective_id=1, has_side_effects=True, vmem_limit_bytes=52 << 20),
         name="mixer",
     )(x, w, taps, rate, bias, gain)
-
-
-def prep_kernel(owner_ref, x_ref, gain_ref, out_ref, scr, inverse):
-    x = x_ref[...].astype(F32)
-    scale = lax.rsqrt(jnp.mean(x * x, axis=-1, keepdims=True) + 1e-6)
-    scr[...] = x * scale * gain_ref[...]
-    for b in range(32):
-        inverse[owner_ref[b]] = b
-    low = lax.broadcasted_iota(jnp.int32, (128, 128), 1) < 64
-
-    def half(block, side):
-        tile = scr[:, pl.ds(pl.multiple_of((block // 2) * 128, 128), 128)]
-        return jnp.where(block % 2 == side, tile, pltpu.roll(tile, 64, axis=1))
-
-    for j in range(16):
-        out_ref[:, j * 128 : (j + 1) * 128] = jnp.where(
-            low, half(inverse[2 * j], 0), half(inverse[2 * j + 1], 1)
-        ).astype(BF16)
-
-
-def prep(owner, x, gain):
-    return pl.pallas_call(
-        prep_kernel,
-        out_shape=jax.ShapeDtypeStruct(x.shape, BF16),
-        in_specs=[
-            pl.BlockSpec(memory_space=pltpu.SMEM),
-            pl.BlockSpec(memory_space=pltpu.VMEM),
-            pl.BlockSpec(memory_space=pltpu.VMEM),
-        ],
-        out_specs=pl.BlockSpec(memory_space=pltpu.VMEM),
-        scratch_shapes=[pltpu.VMEM(x.shape, F32), pltpu.SMEM((32,), jnp.int32)],
-        name="prep",
-    )(owner, x, gain)
-
-
-def finish_kernel(owner_ref, live_ref, x_ref, out_ref, scr):
-    scr[...] = x_ref[...].astype(F32)
-    live = lax.broadcasted_iota(jnp.int32, (128, 128), 0) < live_ref[0]
-    low = lax.broadcasted_iota(jnp.int32, (128, 128), 1) < 64
-
-    def half(block, side):
-        tile = scr[:, pl.ds(pl.multiple_of((block // 2) * 128, 128), 128)]
-        return jnp.where(block % 2 == side, tile, pltpu.roll(tile, 64, axis=1))
-
-    for j in range(16):
-        tile = jnp.where(low, half(owner_ref[2 * j], 0), half(owner_ref[2 * j + 1], 1))
-        out_ref[:, j * 128 : (j + 1) * 128] = jnp.where(live, tile, 0.0).astype(BF16)
-
-
-def finish(owner, live, x):
-    return pl.pallas_call(
-        finish_kernel,
-        out_shape=jax.ShapeDtypeStruct(x.shape, BF16),
-        in_specs=[
-            pl.BlockSpec(memory_space=pltpu.SMEM),
-            pl.BlockSpec(memory_space=pltpu.SMEM),
-            pl.BlockSpec(memory_space=pltpu.VMEM),
-        ],
-        out_specs=pl.BlockSpec(memory_space=pltpu.VMEM),
-        scratch_shapes=[pltpu.VMEM(x.shape, F32)],
-        name="finish",
-    )(owner, live, x)
 
 
 def body(
@@ -320,14 +711,8 @@
         ],
         axis=1,
     )
-    full_rows = lax.all_gather(normed, "tp", axis=0, tiled=True)
-    weights = lax.all_gather(packed, "roll", axis=0, tiled=True)
-    taps = conv_weight.astype(F32).reshape(4, -1)
-    lane_pad = ((0, 0), (0, 124))
-    rate = jnp.pad(decay_rate.reshape(1, -1), lane_pad)
-    bias = jnp.pad(dt_bias.reshape(1, -1), lane_pad)
-    partial = mixer(full_rows, weights, taps, rate, bias, head_gain[None, :])
-    mine = lax.psum_scatter(partial, "tp", scatter_dimension=0, tiled=True)
+    full_rows, weights = gather(normed, packed)
+    mine = mixer(full_rows, weights, conv_weight, decay_rate, dt_bias, head_gain[None, :])
     live = lengths - lax.axis_index("tp") * tok_rows
     return finish(bucket_owner, live, mine)[None]
 

time: 363 us -> 175 us (0.48)
  waiting for transfers between devices: 297 us -> 0 us
  Pallas kernels: 43.8 us -> 166 us
  between operations: 13.8 us -> 0.7 us
    all_gather x2 -> x0, waiting for transfers between devices: 172 us -> none  [the longest x1 105 us: body(): full_rows = lax.all_gather(normed, 'tp', axis=0, tiled=True)]
    reduce_scatter x1 -> x0, waiting for transfers between devices: 125 us -> none  [body(): mine = lax.psum_scatter(partial, 'tp', scatter_dimension=0, tiled=True)]
    pallas_call x0 -> x1, Pallas kernels: none -> 76.1 us  [gather(): pl.pallas_call(gather_kernel, out_shape=(jax.ShapeDtypeStruct((8 * rows.s...]
    pallas_call x1, Pallas kernels: 38.8 us -> 85.2 us  [mixer(): pl.pallas_call(mixer_kernel, grid=(seq // ROWS,), out_shape=jax.ShapeDtyp...]
  transfers between devices with their start and end apart: 3 -> 0, of which waited for: 3 -> 0; matrix products, arithmetic and copies ran while one was open for 2% -> 0% of each run, Pallas kernels for 0% -> 0%
where the time goes in v3:
time: 175 us; the launch traced here: 174 us
  Pallas kernels  166 us (95%)
  local copies, waits for them, and re-layouts  6.05 us (3%)
    pallas_call x1, Pallas kernels, mixer(): pl.pallas_call(mixer_kernel, grid=(seq // ROWS,), out_shape=jax.ShapeDtyp...  85.2 us
    pallas_call x1, Pallas kernels, gather(): pl.pallas_call(gather_kernel, out_shape=(jax.ShapeDtypeStruct((8 * rows.s...  76.1 us
    unnamed x11, local copies, waits for them, and re-layouts  4.33 us

profile of v3, /device:TPU:2, one launch (start us, length us, event | category | flops | bytes accessed | tf_op | source)
XLA Modules:
  0.0 173.9 jit_solution(13522501981614932848)
XLA Ops:
  0.0 0.9 copy.16
  0.9 0.9 copy.17
  1.8 0.8 copy.15
  2.6 0.8 fusion.3.w_ref
  3.3 2.6 %prep.1.x_ref = bf16[128,2048]{1,0:T(8,128)(2,1)} custom-call(s32[32]{0:T(128)} %owner_ref.3, bf16[128,2048]{1,0:T(8,128)(2,1)} %bitcast.12, f32[1,2048]{1,0:T(1,128)} %bitcast.16), custom_call_target="tpu_custom_call" | custom-call | tf_op jit(solution)/shard_map/prep/pallas_call | solution.py:55
  5.9 76.1 %gather.1 = (bf16[1024,2048]{1,0:T(8,128)(2,1)}, bf16[2048,2176]{1,0:T(8,128)(2,1)}) custom-call(bf16[128,2048]{1,0:T(8,128)(2,1)} %prep.1.x_ref, bf16[64,2176]{1,0:T(8,128)(2,1)} %fusion.3.w_ref), custom_call_target="tpu_custom_call" | custom-call | tf_op jit(solution)/shard_map/gather/pallas_call | solution.py:316
  82.1 0.0 copy-start.1
  82.1 0.7 copy-done.1
  82.8 0.0 copy-start.2
  82.8 0.7 copy-done.2
  83.5 0.0 copy-start.3
  83.5 0.7 copy-done.3
  84.1 0.0 copy-start.4
  84.1 0.7 copy-done.4
  84.8 85.2 %mixer.1.x_ref = bf16[128,2048]{1,0:T(8,128)(2,1)S(1)} custom-call(bf16[1024,2048]{1,0:T(8,128)(2,1)} %get-tuple-element.7.x_ref, bf16[2048,2176]{1,0:T(8,128)(2,1)} %get-tuple-element.8.w_ref, bf16[4,4,256]{2,1,0:T(4,128)(2,1)S(1)} %copy-done.1, f32[2,2]{1,0:T(2,128)S(1)} %copy-done.2, f32[2,2]{1,0:T(2,128)S(1)} %copy-done.3, f32[1,128]{1,0:T(1,128)S(1)} %bitcast.10), custom_call_target="tpu_custom_call" | custom-call | tf_op jit(solution)/shard_map/mixer/pallas_call | solution.py:658
  170.0 0.0 copy-start
  170.0 0.8 copy-done
  171.5 2.5 %finish.1 = bf16[128,2048]{1,0:T(8,128)(2,1)} custom-call(s32[32]{0:T(128)} %owner_ref.3, s32[1]{0:T(128)S(6)} %sub.7.live_ref, bf16[128,2048]{1,0:T(8,128)(2,1)} %copy-done), custom_call_target="tpu_custom_call" | custom-call | tf_op jit(solution)/shard_map/finish/pallas_call | solution.py:84
Async XLA Ops:
  82.1 0.7 copy-start.1
  82.8 0.7 copy-start.2
  83.5 0.7 copy-start.3
  84.1 0.7 copy-start.4
  170.0 0.8 copy-start

commit v4 on v3

--- a/solution.py
+++ b/solution.py
@@ -124,213 +124,291 @@
     pl.semaphore_wait(barrier, len(devices))
 
 
-def gather_kernel(x_ref, w_ref, xo, wo, transit, zs_up, zs_dn, zr, ws, wr, ys, yr, own_sem):
-    me = Place()
-    left_x, right_x = me.at(x=(me.x + 3) % 4), me.at(x=(me.x + 1) % 4)
-    left_y, right_y = me.at(y=(me.y + 3) % 4), me.at(y=(me.y + 1) % 4)
-    up, down = me.at(zl=(me.zl + 1) % 4), me.at(zl=(me.zl + 3) % 4)
-    sibling, partner = me.at(core=1 - me.core), me.at(zh=1 - me.zh)
-    behind, ahead = me.along_z(6), me.along_z(2)
-    outer = (me.zh * 4 + me.zl + 2) % 8 < 4
-    meet([left_x, right_x, left_y, right_y, up, down, sibling, partner, behind, ahead])
-
-    def copy(src, dst, send, recv, device):
+class Pull:
+    def __init__(self, x_ref, w_refs, xo, wos, transit, zs_up, zs_dn, zr, ws, wr, ys, yr, own_sem):
+        self.x_ref, self.w_refs, self.xo, self.wos, self.transit = x_ref, w_refs, xo, wos, transit
+        self.zs_up, self.zs_dn, self.zr, self.ws, self.wr = zs_up, zs_dn, zr, ws, wr
+        self.ys, self.yr, self.own_sem = ys, yr, own_sem
+        me = self.me = Place()
+        self.xl, self.xr, self.xf = (me.x + 3) % 4, (me.x + 1) % 4, (me.x + 2) % 4
+        self.yl, self.yn, self.yf = (me.y + 3) % 4, (me.y + 1) % 4, (me.y + 2) % 4
+        self.left_x, self.right_x = me.at(x=self.xl), me.at(x=self.xr)
+        self.left_y, self.right_y = me.at(y=self.yl), me.at(y=self.yn)
+        self.up, self.down = me.at(zl=(me.zl + 1) % 4), me.at(zl=(me.zl + 3) % 4)
+        self.sibling, self.partner = me.at(core=1 - me.core), me.at(zh=1 - me.zh)
+        self.behind, self.ahead = me.along_z(6), me.along_z(2)
+        self.away_to = me.along_z(jnp.where(me.zh == 0, 6, 2))
+        self.outer = (me.zh * 4 + me.zl + 2) % 8 < 4
+        self.other = 1 - me.zh
+        order = [[0, 1, 2, 3], [1, 2, 0, 3], [2, 1, 3, 0], [3, 2, 1, 0]]
+        self.slot = [
+            jnp.where(
+                me.zl == 0,
+                order[0][j],
+                jnp.where(me.zl == 1, order[1][j], jnp.where(me.zl == 2, order[2][j], order[3][j])),
+            )
+            for j in range(4)
+        ]
+
+    def meet(self):
+        meet(
+            [self.left_x, self.right_x, self.left_y, self.right_y, self.up, self.down]
+            + [self.sibling, self.partner, self.behind, self.ahead]
+        )
+
+    def copy(self, src, dst, send, recv, device):
         return pltpu.make_async_remote_copy(
             src_ref=src, dst_ref=dst, send_sem=send, recv_sem=recv, device_id=device, device_id_type=MESH
         )
 
-    sent = []
-
-    def send(src, dst, sems, i, device):
-        c = copy(src, dst, sems[0].at[i], sems[1].at[i], device)
-        c.start()
-        sent.append(c)
-
-    def arrived(dst, sems, i):
-        copy(dst, dst, sems[0].at[i], sems[1].at[i], sibling).wait_recv()
-
-    W, Y = (ws, wr), (ys, yr)
-
-    def shard(zl, x, core):
-        return wo.at[pl.ds(pl.multiple_of((zl * 8 + x * 2 + core) * 64, 64), 64)]
-
-    def part(zl, x, core, p):
-        return wo.at[pl.ds(pl.multiple_of((zl * 8 + x * 2 + core) * 64 + p * 32, 32), 32)]
-
-    def block(zh, y, p):
-        return xo.at[pl.ds(pl.multiple_of((zh * 4 + y) * 128 + p * 64, 64), 64)]
-
-    order = [[0, 1, 2, 3], [1, 2, 0, 3], [2, 1, 3, 0], [3, 2, 1, 0]]
-    slot = [
-        jnp.where(me.zl == 0, order[0][j], jnp.where(me.zl == 1, order[1][j], jnp.where(me.zl == 2, order[2][j], order[3][j])))
-        for j in range(4)
-    ]
-    xl, xr = (me.x + 3) % 4, (me.x + 1) % 4
-    xf = (me.x + 2) % 4
-    yl, yr_, yf = (me.y + 3) % 4, (me.y + 1) % 4, (me.y + 2) % 4
-    mine_x = [x_ref.at[pl.ds(p * 64, 64)] for p in range(2)]
-
-    def z_up(src, z):
-        return copy(src, shard(z, me.x, me.core), zs_up.at[z], zr.at[z], up)
-
-    def z_down(src, z):
-        return copy(src, shard(z, me.x, me.core), zs_dn.at[z], zr.at[z], down)
-
-    def spread_x(src, j):
-        z = slot[j]
-        for i, device in ((0, right_x), (1, left_x)):
-            send(src, shard(z, me.x, me.core), W, j * 8 + i, device)
-        send(src, shard(z, me.x, me.core), W, j * 8 + 4, sibling)
-
-    def relay_x(j):
-        z = slot[j]
-        arrived(shard(z, xl, me.core), W, j * 8)
-        send(part(z, xl, me.core, 0), part(z, xl, me.core, 0), W, j * 8 + 2, right_x)
-        arrived(shard(z, xr, me.core), W, j * 8 + 1)
-        send(part(z, xr, me.core, 1), part(z, xr, me.core, 1), W, j * 8 + 3, left_x)
-        send(shard(z, xl, me.core), shard(z, xl, me.core), W, j * 8 + 5, sibling)
-        send(shard(z, xr, me.core), shard(z, xr, me.core), W, j * 8 + 6, sibling)
-
-    def far_x(j):
-        z = slot[j]
-        arrived(part(z, xf, me.core, 0), W, j * 8 + 2)
-        arrived(part(z, xf, me.core, 1), W, j * 8 + 3)
-        send(shard(z, xf, me.core), shard(z, xf, me.core), W, j * 8 + 7, sibling)
-
-    def take_z(j):
-        z = slot[j]
-        copy(shard(z, me.x, me.core), shard(z, me.x, me.core), zs_up.at[z], zr.at[z], up).wait_recv()
-
-        @pl.when((z < me.zl) & (me.zl < 3))
+    def shard(self, w, z, x, core):
+        return self.wos[w].at[pl.ds(pl.multiple_of((z * 8 + x * 2 + core) * 64, 64), 64)]
+
+    def part(self, w, z, x, core, p):
+        return self.wos[w].at[pl.ds(pl.multiple_of((z * 8 + x * 2 + core) * 64 + p * 32, 32), 32)]
+
+    def z_copy(self, w, z, src, upward):
+        i = w * 4 + z
+        dst = self.shard(w, z, self.me.x, self.me.core)
+        sems, device = (self.zs_up, self.up) if upward else (self.zs_dn, self.down)
+        return self.copy(src, dst, sems.at[i], self.zr.at[i], device)
+
+    def start_z(self, w):
+        for upward, has in ((True, self.me.zl < 3), (False, self.me.zl > 0)):
+
+            @pl.when(has)
+            def _():
+                self.z_copy(w, self.me.zl, self.w_refs[w], upward).start()
+
+    def take_z(self, w, j):
+        me, z = self.me, self.slot[j]
+        here = self.shard(w, z, me.x, me.core)
+        self.z_copy(w, z, here, True).wait_recv()
+        for upward, on in ((True, (z < me.zl) & (me.zl < 3)), (False, (z > me.zl) & (me.zl > 0))):
+
+            @pl.when(on)
+            def _():
+                self.z_copy(w, z, self.shard(w, z, me.x, me.core), upward).start()
+
+    def w_msg(self, w, j, i):
+        me, z = self.me, self.slot[j]
+        own = self.shard(w, z, me.x, me.core)
+        src, dst, device = (
+            (self.w_refs[w] if j == 0 else own, own, self.right_x),
+            (self.w_refs[w] if j == 0 else own, own, self.left_x),
+            (self.part(w, z, self.xl, me.core, 0),) * 2 + (self.right_x,),
+            (self.part(w, z, self.xr, me.core, 1),) * 2 + (self.left_x,),
+            (self.w_refs[w] if j == 0 else own, own, self.sibling),
+            (self.shard(w, z, self.xl, me.core),) * 2 + (self.sibling,),
+            (self.shard(w, z, self.xr, me.core),) * 2 + (self.sibling,),
+            (self.shard(w, z, self.xf, me.core),) * 2 + (self.sibling,),
+        )[i]
+        n = w * 32 + j * 8 + i
+        return self.copy(src, dst, self.ws.at[n], self.wr.at[n], device)
+
+    def w_wait(self, w, j, i):
+        me, z = self.me, self.slot[j]
+        dst = (
+            lambda: self.shard(w, z, self.xl, me.core),
+            lambda: self.shard(w, z, self.xr, me.core),
+            lambda: self.part(w, z, self.xf, me.core, 0),
+            lambda: self.part(w, z, self.xf, me.core, 1),
+            lambda: self.shard(w, z, me.x, 1 - me.core),
+            lambda: self.shard(w, z, self.xl, 1 - me.core),
+            lambda: self.shard(w, z, self.xr, 1 - me.core),
+            lambda: self.shard(w, z, self.xf, 1 - me.core),
+        )[i]()
+        n = w * 32 + j * 8 + i
+        self.copy(dst, dst, self.ws.at[n], self.wr.at[n], self.sibling).wait_recv()
+
+    def spread_x(self, w, j):
+        for i in (0, 1, 4):
+            self.w_msg(w, j, i).start()
+
+    def relay_x(self, w, j):
+        self.w_wait(w, j, 0)
+        self.w_msg(w, j, 2).start()
+        self.w_wait(w, j, 1)
+        self.w_msg(w, j, 3).start()
+        self.w_msg(w, j, 5).start()
+        self.w_msg(w, j, 6).start()
+
+    def far_x(self, w, j):
+        self.w_wait(w, j, 2)
+        self.w_wait(w, j, 3)
+        self.w_msg(w, j, 7).start()
+
+    def siblings(self, w):
+        for j in range(4):
+            for i in range(4, 8):
+                self.w_wait(w, j, i)
+
+    def block(self, zh, y, p):
+        return self.xo.at[pl.ds(pl.multiple_of((zh * 4 + y) * 128 + p * 64, 64), 64)]
+
+    def y_msg(self, b, k):
+        me = self.me
+        zh = self.other if b else me.zh
+        if k < 4:
+            dst = self.block(zh, me.y, k % 2)
+            src = dst if b else self.x_ref.at[pl.ds(k % 2 * 64, 64)]
+            device = self.right_y if k < 2 else self.left_y
+        else:
+            dst = src = self.block(zh, self.yl if k == 4 else self.yn, k - 4)
+            device = self.right_y if k == 4 else self.left_y
+        return self.copy(src, dst, self.ys.at[b * 6 + k], self.yr.at[b * 6 + k], device)
+
+    def y_wait(self, b, k):
+        zh = self.other if b else self.me.zh
+        y, p = ((self.yl, 0), (self.yl, 1), (self.yn, 0), (self.yn, 1), (self.yf, 0), (self.yf, 1))[k]
+        dst = self.block(zh, y, p)
+        self.copy(dst, dst, self.ys.at[b * 6 + k], self.yr.at[b * 6 + k], self.partner).wait_recv()
+
+    def relay_y(self, b):
+        self.y_wait(b, 0)
+        self.y_msg(b, 4).start()
+        self.y_wait(b, 3)
+        self.y_msg(b, 5).start()
+
+    def rest_y(self, b):
+        for k in (1, 2, 4, 5):
+            self.y_wait(b, k)
+
+    def direct(self):
+        return self.copy(
+            self.x_ref.at[pl.ds(0, 64)], self.block(self.me.zh, self.me.y, 0), self.ys.at[12], self.yr.at[12], self.partner
+        )
+
+    def away(self):
+        i = 13 + 2 * self.me.zh
+        return self.copy(
+            self.x_ref.at[pl.ds(64, 64)], self.transit.at[self.me.zh], self.ys.at[i], self.yr.at[i], self.away_to
+        )
+
+    def onward(self, s):
+        i = 14 + 2 * s
+        return self.copy(
+            self.transit.at[s], self.block(s, self.me.y, 1), self.ys.at[i], self.yr.at[i], self.ahead if s else self.behind
+        )
+
+    def pass_on(self):
+        @pl.when(self.outer)
         def _():
-            z_up(shard(z, me.x, me.core), z).start()
-
-        @pl.when((z > me.zl) & (me.zl > 0))
+            for s in range(2):
+                i = 13 + 2 * s
+                dst = self.transit.at[s]
+                self.copy(dst, dst, self.ys.at[i], self.yr.at[i], self.partner).wait_recv()
+                self.onward(s).start()
+
+    def take_other(self, p):
+        i = 14 + 2 * self.other if p else 12
+        dst = self.block(self.other, self.me.y, p)
+        self.copy(dst, dst, self.ys.at[i], self.yr.at[i], self.partner).wait_recv()
+        self.y_msg(1, p).start()
+        self.y_msg(1, 2 + p).start()
+
+    def open(self):
+        me = self.me
+        self.meet()
+        self.start_z(0)
+        self.spread_x(0, 0)
+        self.away().start()
+        self.direct().start()
+        for k in (0, 2, 1, 3):
+            self.y_msg(0, k).start()
+        keep = [
+            pltpu.make_async_copy(self.w_refs[w], self.shard(w, me.zl, me.x, me.core), self.own_sem.at[w])
+            for w in range(2)
+        ]
+        rows = pl.ds(pl.multiple_of((me.zh * 4 + me.y) * 128, 128), 128)
+        keep.append(pltpu.make_async_copy(self.x_ref, self.xo.at[rows], self.own_sem.at[2]))
+        for c in keep:
+            c.start()
+        for j in (1, 2, 3):
+            self.take_z(0, j)
+            self.spread_x(0, j)
+            self.relay_x(0, j - 1)
+            if j == 2:
+                self.relay_y(0)
+                self.pass_on()
+        self.start_z(1)
+        self.far_x(0, 0)
+        self.take_other(0)
+        self.far_x(0, 1)
+        self.take_other(1)
+        self.relay_x(0, 3)
+        self.take_z(1, 1)
+        self.far_x(0, 2)
+        self.take_z(1, 2)
+
+        @pl.when(me.zh == 1)
         def _():
-            z_down(shard(z, me.x, me.core), z).start()
-
-        spread_x(shard(z, me.x, me.core), j)
-
-    def spread_y(src, zh, b, p):
-        send(src, block(zh, me.y, p), Y, b * 6 + p, right_y)
-        send(src, block(zh, me.y, p), Y, b * 6 + 2 + p, left_y)
-
-    def relay_y(zh, b):
-        arrived(block(zh, yl, 0), Y, b * 6)
-        send(block(zh, yl, 0), block(zh, yl, 0), Y, b * 6 + 4, right_y)
-        arrived(block(zh, yr_, 1), Y, b * 6 + 3)
-        send(block(zh, yr_, 1), block(zh, yr_, 1), Y, b * 6 + 5, left_y)
-
-    def rest_y(zh, b):
-        arrived(block(zh, yl, 1), Y, b * 6 + 1)
-        arrived(block(zh, yr_, 0), Y, b * 6 + 2)
-        arrived(block(zh, yf, 0), Y, b * 6 + 4)
-        arrived(block(zh, yf, 1), Y, b * 6 + 5)
-
-    other = 1 - me.zh
-
-    def away():
-        i = 13 + 2 * me.zh
-        return copy(mine_x[1], transit.at[me.zh], ys.at[i], yr.at[i], me.along_z(jnp.where(me.zh == 0, 6, 2)))
-
-    def onward(s):
-        i = 14 + 2 * s
-        return copy(transit.at[s], block(s, me.y, 1), ys.at[i], yr.at[i], ahead if s else behind)
-
-
-    @pl.when(me.zl < 3)
-    def _():
-        z_up(w_ref, me.zl).start()
-
-    @pl.when(me.zl > 0)
-    def _():
-        z_down(w_ref, me.zl).start()
-
-    spread_x(w_ref, 0)
-    away().start()
-    send(mine_x[0], block(me.zh, me.y, 0), Y, 12, partner)
-    spread_y(mine_x[0], me.zh, 0, 0)
-    spread_y(mine_x[1], me.zh, 0, 1)
-    keep_w = pltpu.make_async_copy(w_ref, shard(me.zl, me.x, me.core), own_sem.at[0])
-    keep_w.start()
-    keep_x = pltpu.make_async_copy(x_ref, xo.at[pl.ds(pl.multiple_of((me.zh * 4 + me.y) * 128, 128), 128)], own_sem.at[1])
-    keep_x.start()
-
-    take_z(1)
-    relay_x(0)
-    take_z(2)
-    relay_y(me.zh, 0)
-
-    @pl.when(outer)
-    def _():
-        for s in range(2):
-            arrived(transit.at[s], Y, 13 + 2 * s)
-            onward(s).start()
-
-    relay_x(1)
-    take_z(3)
-    far_x(0)
-    relay_x(2)
-    arrived(block(other, me.y, 0), Y, 12)
-    spread_y(block(other, me.y, 0), other, 1, 0)
-    far_x(1)
-    arrived(block(other, me.y, 1), Y, 14 + 2 * other)
-    spread_y(block(other, me.y, 1), other, 1, 1)
-    relay_x(3)
-    far_x(2)
-    relay_y(other, 1)
-    far_x(3)
-    rest_y(me.zh, 0)
-    rest_y(other, 1)
-    for j in range(4):
-        z = slot[j]
-        for i, x in ((4, me.x), (5, xl), (6, xr), (7, xf)):
-            arrived(shard(z, x, 1 - me.core), W, j * 8 + i)
-    keep_w.wait()
-    keep_x.wait()
-    for c in sent:
-        c.wait_send()
-    away().wait_send()
-
-    @pl.when(outer)
-    def _():
-        for s in range(2):
-            onward(s).wait_send()
-
-    for j in range(4):
-        z = slot[j]
-
-        @pl.when((z <= me.zl) & (me.zl < 3))
+            self.relay_y(1)
+
+        self.far_x(0, 3)
+        self.take_z(1, 3)
+        for j in range(4):
+            self.spread_x(1, j)
+
+        @pl.when(me.zh == 0)
         def _():
-            z_up(shard(z, me.x, me.core), z).wait_send()
-
-        @pl.when((z >= me.zl) & (me.zl > 0))
+            self.rest_y(0)
+
+        @pl.when(me.zh == 1)
         def _():
-            z_down(shard(z, me.x, me.core), z).wait_send()
+            self.rest_y(1)
+
+        self.siblings(0)
+        for c in keep:
+            c.wait()
+
+    def second(self):
+        @pl.when(self.me.zh == 0)
+        def _():
+            self.relay_y(1)
+
+        for j in range(4):
+            self.relay_x(1, j)
+
+    def third(self):
+        for j in range(4):
+            self.far_x(1, j)
+
+    def later_half(self):
+        @pl.when(self.me.zh == 0)
+        def _():
+            self.rest_y(1)
+
+        @pl.when(self.me.zh == 1)
+        def _():
+            self.rest_y(0)
+
+    def close(self):
+        me = self.me
+        for w in range(2):
+            for j in range(4):
+                z = self.slot[j]
+                for i in range(8):
+                    self.w_msg(w, j, i).wait_send()
+                for upward, on in ((True, (z <= me.zl) & (me.zl < 3)), (False, (z >= me.zl) & (me.zl > 0))):
+
+                    @pl.when(on)
+                    def _():
+                        self.z_copy(w, z, self.shard(w, z, me.x, me.core), upward).wait_send()
+
+        for b in range(2):
+            for k in range(6):
+                self.y_msg(b, k).wait_send()
+        self.direct().wait_send()
+        self.away().wait_send()
+
+        @pl.when(self.outer)
+        def _():
+            for s in range(2):
+                self.onward(s).wait_send()
 
 
 DMA = pltpu.SemaphoreType.DMA
-
-
-def gather(rows, packed):
-    return pl.pallas_call(
-        gather_kernel,
-        out_shape=(
-            jax.ShapeDtypeStruct((8 * rows.shape[0], rows.shape[1]), BF16),
-            jax.ShapeDtypeStruct((32 * packed.shape[0], packed.shape[1]), BF16),
-        ),
-        in_specs=[pl.BlockSpec(memory_space=pl.ANY)] * 2,
-        out_specs=(pl.BlockSpec(memory_space=pl.ANY),) * 2,
-        scratch_shapes=[
-            pltpu.VMEM((2, 64, 2048), BF16),
-            DMA((4,)), DMA((4,)), DMA((4,)),
-            DMA((32,)), DMA((32,)),
-            DMA((17,)), DMA((17,)),
-            DMA((2,)),
-        ],
-        compiler_params=pltpu.CompilerParams(collective_id=0, has_side_effects=True),
-        name="gather",
-    )(rows, packed)
 
 
 class Sums:
@@ -342,9 +420,6 @@
         self.left, self.right = me.at(y=(me.y + 3) % 4), me.at(y=(me.y + 1) % 4)
         self.partner, self.behind, self.ahead = me.at(zh=1 - me.zh), me.along_z(6), me.along_z(2)
         self.outer = (me.zh * 4 + me.zl + 2) % 8 < 4
-
-    def meet(self):
-        meet([self.left, self.right, self.partner, self.behind, self.ahead])
 
     def copy(self, i, src, dst, device):
         return pltpu.make_async_remote_copy(
@@ -437,19 +512,29 @@
 
 
 def mixer_kernel(
-    x_ref, w_ref, taps_ref, rate_ref, bias_ref, gain_ref, out_ref,
+    own_ref, w1_ref, w2_ref, taps_ref, rate_ref, bias_ref, gain_ref, out_ref,
+    x_ref, w_ref, wout_ref, hid, passing, zs_up, zs_dn, zr, ws, wr, ys, yr, own_sem,
     pscr, oscr, state, p_ref, first, full, mixed, kept, summed, landed, transit, ss, rs,
 ):
     step = pl.program_id(0)
     across = Sums(p_ref, first, full, mixed, kept, summed, landed, transit, ss, rs)
 
+    pull = Pull(
+        own_ref, (w1_ref, w2_ref), x_ref, (w_ref, wout_ref), passing, zs_up, zs_dn, zr, ws, wr, ys, yr, own_sem
+    )
+
     @pl.when(step == 0)
     def _():
-        across.meet()
+        pull.open()
+
+    @pl.when(step == 1)
+    def _():
+        pull.second()
 
     @pl.when(step == 2)
     def _():
         across.begin(0)
+        pull.later_half()
 
 
     @pl.when(step == 0)
@@ -461,9 +546,15 @@
     def _():
         pscr[0:8, :] = pscr[ROWS : ROWS + 8, :]
 
-    x = x_ref[...]
+    here = pl.ds(pl.multiple_of(step * ROWS, ROWS), ROWS)
+    x = x_ref[here, :]
     gates = mm(x, w_ref[:, 1536:1664])
     pscr[8 : 8 + ROWS, :] = mm(x, w_ref[:, 0:1024])
+
+    @pl.when(step == 1)
+    def _():
+        pull.third()
+
 
     lane = lax.broadcasted_iota(jnp.int32, (1, 128), 1)
     rate, bias = jnp.zeros((1, 128), F32), jnp.zeros((1, 128), F32)
@@ -635,7 +726,16 @@
         r = r * lax.rsqrt(jnp.mean(r * r, axis=-1, keepdims=True) + 1e-6) * gain_ref[...]
         hidden.append((r * silu(og[:, n * 128 : (n + 1) * 128])).astype(BF16))
     hidden = jnp.concatenate(hidden, axis=1)
-    p_ref[pl.ds(pl.multiple_of(step * ROWS, ROWS), ROWS), :] = mm_nt(hidden, w_ref[:, 1664:2176]).astype(BF16)
+    hid[here, :] = hidden
+
+    @pl.when(step == 1)
+    def _():
+        pull.siblings(1)
+        p_ref[0:ROWS, :] = mm_nt(hid[0:ROWS, :], wout_ref[...]).astype(BF16)
+
+    @pl.when(step > 0)
+    def _():
+        p_ref[here, :] = mm_nt(hid[here, :], wout_ref[...]).astype(BF16)
 
     @pl.when(step == 2)
     def _():
@@ -650,25 +750,37 @@
         across.total(1)
         across.pass_on(1)
         across.finish(out_ref)
-
-
-def mixer(x, w, taps, rate, bias, gain):
-    seq, width = x.shape
+        pull.close()
+
+
+def mixer(rows, w1, w2, taps, rate, bias, gain):
+    own, width = rows.shape
+    seq, depth = own * 8, w1.shape[0] * 32
     whole = lambda i: (0, 0)
     return pl.pallas_call(
         mixer_kernel,
         grid=(seq // ROWS,),
-        out_shape=jax.ShapeDtypeStruct((seq // 8, width), BF16),
+        out_shape=jax.ShapeDtypeStruct(rows.shape, BF16),
         in_specs=[
-            pl.BlockSpec((ROWS, 2048), lambda i: (i, 0)),
-            pl.BlockSpec((2048, 2176), whole, pipeline_mode=pl.Buffered(1)),
+            pl.BlockSpec(memory_space=pl.ANY),
+            pl.BlockSpec(memory_space=pl.ANY),
+            pl.BlockSpec(memory_space=pl.ANY),
             pl.BlockSpec((4, 4, 256), lambda i: (0, 0, 0)),
             pl.BlockSpec(memory_space=pltpu.SMEM),
             pl.BlockSpec(memory_space=pltpu.SMEM),
             pl.BlockSpec((1, 128), whole),
         ],
-        out_specs=pl.BlockSpec((seq // 8, width), whole),
+        out_specs=pl.BlockSpec(rows.shape, whole),
         scratch_shapes=[
+            pltpu.VMEM((seq, width), BF16),
+            pltpu.VMEM((depth, w1.shape[1]), BF16),
+            pltpu.VMEM((depth, w2.shape[1]), BF16),
+            pltpu.VMEM((seq, 512), BF16),
+            pltpu.VMEM((2, 64, width), BF16),
+            DMA((8,)), DMA((8,)), DMA((8,)),
+            DMA((64,)), DMA((64,)),
+            DMA((17,)), DMA((17,)),
+            DMA((3,)),
             pltpu.VMEM((ROWS + 8, 1024), F32),
             pltpu.VMEM((ROWS, 512), F32),
             pltpu.VMEM((2, 128, 256), F32),
@@ -682,9 +794,9 @@
             pltpu.VMEM((2, 64, width), BF16),
             DMA((17,)), DMA((17,)),
         ],
-        compiler_params=pltpu.CompilerParams(collective_id=1, has_side_effects=True, vmem_limit_bytes=52 << 20),
+        compiler_params=pltpu.CompilerParams(collective_id=0, has_side_effects=True, vmem_limit_bytes=58 << 20),
         name="mixer",
-    )(x, w, taps, rate, bias, gain)
+    )(rows, w1, w2, taps, rate, bias, gain)
 
 
 def body(
@@ -704,15 +816,11 @@
     rows = w_in.shape[0]
     normed = prep(bucket_owner, prompt_states[0], in_gain[None, :])
     packed = jnp.concatenate(
-        [
-            w_in.reshape(rows, -1),
-            jnp.pad(w_gates.reshape(rows, -1), ((0, 0), (0, 120))),
-            out_weight.reshape(rows, -1),
-        ],
-        axis=1,
+        [w_in.reshape(rows, -1), jnp.pad(w_gates.reshape(rows, -1), ((0, 0), (0, 120)))], axis=1
     )
-    full_rows, weights = gather(normed, packed)
-    mine = mixer(full_rows, weights, conv_weight, decay_rate, dt_bias, head_gain[None, :])
+    mine = mixer(
+        normed, packed, out_weight.reshape(rows, -1), conv_weight, decay_rate, dt_bias, head_gain[None, :]
+    )
     live = lengths - lax.axis_index("tp") * tok_rows
     return finish(bucket_owner, live, mine)[None]
 

time: 175 us -> 166 us (0.949)
  Pallas kernels: 166 us -> 161 us
  local copies, waits for them, and re-layouts: 6.05 us -> 1.56 us
    pallas_call x1 -> x0, Pallas kernels: 76.1 us -> none  [gather(): pl.pallas_call(gather_kernel, out_shape=(jax.ShapeDtypeStruct((8 * rows.s...]
    pallas_call x1, Pallas kernels: 85.2 us -> 156 us  [mixer(): pl.pallas_call(mixer_kernel, grid=(seq // ROWS,), out_shape=jax.ShapeDtyp...]
    unnamed x11 -> x7, local copies, waits for them, and re-layouts: 4.33 us -> 1.45 us
where the time goes in v4:
time: 166 us; the launch traced here: 164 us
  Pallas kernels  161 us (97%)
    pallas_call x1, Pallas kernels, mixer(): pl.pallas_call(mixer_kernel, grid=(seq // ROWS,), out_shape=jax.ShapeDtyp...  156 us

profile of v4, /device:TPU:2, one launch (start us, length us, event | category | flops | bytes accessed | tf_op | source)
XLA Modules:
  0.0 163.9 jit_solution(1790196890656844013)
XLA Ops:
  0.0 0.0 copy-start
  0.0 2.6 %prep.1.own_ref = bf16[128,2048]{1,0:T(8,128)(2,1)} custom-call(s32[32]{0:T(128)} %owner_ref.3, bf16[128,2048]{1,0:T(8,128)(2,1)} %bitcast.11, f32[1,2048]{1,0:T(1,128)} %bitcast.15), custom_call_target="tpu_custom_call" | custom-call | tf_op jit(solution)/shard_map/prep/pallas_call | solution.py:55
  2.6 0.0 copy-done
  2.6 0.0 copy-start.2
  2.7 0.7 copy-done.2
  3.3 0.1 copy.15
  3.4 0.0 copy-start.1
  3.4 0.7 fusion.1.w1_ref
  4.1 0.1 copy-done.1
  4.3 0.6 copy.17
  4.9 155.8 %mixer.1.x_ref = bf16[128,2048]{1,0:T(8,128)(2,1)} custom-call(bf16[128,2048]{1,0:T(8,128)(2,1)} %prep.1.own_ref, bf16[64,1664]{1,0:T(8,128)(2,1)} %fusion.1.w1_ref, bf16[64,512]{1,0:T(8,128)(2,1)} %bitcast.12, bf16[4,4,256]{2,1,0:T(4,128)(2,1)} %taps_ref.1, f32[2,2]{1,0:T(2,128)} %rate_ref.1, f32[2,2]{1,0:T(2,128)} %bias_ref.1, f32[1,128]{1,0:T(1,128)} %bitcast.17), custom_call_target="tpu_custom_call" | custom-call | tf_op jit(solution)/shard_map/mixer/pallas_call | solution.py:760
  161.4 2.5 %finish.1 = bf16[128,2048]{1,0:T(8,128)(2,1)} custom-call(s32[32]{0:T(128)} %owner_ref.3, s32[1]{0:T(128)S(6)} %sub.7.live_ref, bf16[128,2048]{1,0:T(8,128)(2,1)} %mixer.1.x_ref), custom_call_target="tpu_custom_call" | custom-call | tf_op jit(solution)/shard_map/finish/pallas_call | solution.py:84
  (1 shorter events, 0.0 us)
Async XLA Ops:
  0.0 2.6 %copy-start = (bf16[64,6,256]{2,0,1:T(8,128)(2,1)S(1)}, bf16[64,6,256]{2,0,1:T(8,128)(2,1)}, u32[]{:S(2)}) copy-start(bf16[64,6,256]{2,0,1:T(8,128)(2,1)} %param.14) | copy-start | bytes 589828
  2.6 0.7 copy-start.2
  3.4 0.8 copy-start.1

commit v5 on v4

--- a/solution.py
+++ b/solution.py
@@ -446,12 +446,31 @@
         for k in range(4):
             self.message(b, k).start()
 
+    def begin_blocks(self, b, upper):
+        y = self.me.y
+        for k, block in enumerate(((y + 2) % 4, (y + 2) % 4, (y + 1) % 4, (y + 3) % 4)):
+
+            @pl.when((block >= 2) if upper else (block < 2))
+            def _():
+                self.message(b, k).start()
+
+    def relay_part(self, b, p, near):
+        self.message(b, p).wait_recv()
+        self.mixed[b, p] = (self.half(b, near, p)[...].astype(F32) + self.first[b, p].astype(F32)).astype(BF16)
+        self.message(b, 4 + p).start()
+
     def relay(self, b):
         y = self.me.y
         for p, near in ((0, (y + 1) % 4), (1, (y + 3) % 4)):
-            self.message(b, p).wait_recv()
-            self.mixed[b, p] = (self.half(b, near, p)[...].astype(F32) + self.first[b, p].astype(F32)).astype(BF16)
-            self.message(b, 4 + p).start()
+            self.relay_part(b, p, near)
+
+    def relay_blocks(self, b, upper):
+        y = self.me.y
+        for p, near in ((0, (y + 1) % 4), (1, (y + 3) % 4)):
+
+            @pl.when((near >= 2) if upper else (near < 2))
+            def _():
+                self.relay_part(b, p, near)
 
     def across(self, b, p):
         if p == 0:
@@ -728,6 +747,7 @@
     hidden = jnp.concatenate(hidden, axis=1)
     hid[here, :] = hidden
 
+
     @pl.when(step == 1)
     def _():
         pull.siblings(1)
@@ -740,12 +760,14 @@
     @pl.when(step == 2)
     def _():
         across.relay(0)
+        across.begin_blocks(1, False)
 
     @pl.when(step == 3)
     def _():
-        across.begin(1)
+        across.begin_blocks(1, True)
+        across.relay_blocks(1, False)
         across.total(0)
-        across.relay(1)
+        across.relay_blocks(1, True)
         across.pass_on(0)
         across.total(1)
         across.pass_on(1)

time: 166 us -> 169 us (1.018)
  the two profiles are of different devices: /device:TPU:2 before, /device:TPU:161 now
where the time goes in v5:
time: 169 us
  Pallas kernels  166 us (98%)
    pallas_call x1, Pallas kernels, mixer(): pl.pallas_call(mixer_kernel, grid=(seq // ROWS,), out_shape=jax.ShapeDtyp...  161 us

profile of v5, /device:TPU:161, one launch (start us, length us, event | category | flops | bytes accessed | tf_op | source)
XLA Modules:
  0.0 168.7 jit_solution(7046782362726500207)
XLA Ops:
  0.0 0.0 copy-start
  0.0 2.6 %prep.1.own_ref = bf16[128,2048]{1,0:T(8,128)(2,1)} custom-call(s32[32]{0:T(128)} %owner_ref.3, bf16[128,2048]{1,0:T(8,128)(2,1)} %bitcast.11, f32[1,2048]{1,0:T(1,128)} %bitcast.15), custom_call_target="tpu_custom_call" | custom-call | tf_op jit(solution)/shard_map/prep/pallas_call | solution.py:55
  2.6 0.0 copy-done
  2.6 0.0 copy-start.2
  2.7 0.7 copy-done.2
  3.3 0.1 copy.15
  3.4 0.0 copy-start.1
  3.4 0.7 fusion.1.w1_ref
  4.1 0.1 copy-done.1
  4.3 0.6 copy.17
  4.9 160.7 %mixer.1.x_ref = bf16[128,2048]{1,0:T(8,128)(2,1)} custom-call(bf16[128,2048]{1,0:T(8,128)(2,1)} %prep.1.own_ref, bf16[64,1664]{1,0:T(8,128)(2,1)} %fusion.1.w1_ref, bf16[64,512]{1,0:T(8,128)(2,1)} %bitcast.12, bf16[4,4,256]{2,1,0:T(4,128)(2,1)} %taps_ref.1, f32[2,2]{1,0:T(2,128)} %rate_ref.1, f32[2,2]{1,0:T(2,128)} %bias_ref.1, f32[1,128]{1,0:T(1,128)} %bitcast.17), custom_call_target="tpu_custom_call" | custom-call | tf_op jit(solution)/shard_map/mixer/pallas_call | solution.py:782
  166.2 2.5 %finish.1 = bf16[128,2048]{1,0:T(8,128)(2,1)} custom-call(s32[32]{0:T(128)} %owner_ref.3, s32[1]{0:T(128)S(6)} %sub.7.live_ref, bf16[128,2048]{1,0:T(8,128)(2,1)} %mixer.1.x_ref), custom_call_target="tpu_custom_call" | custom-call | tf_op jit(solution)/shard_map/finish/pallas_call | solution.py:84
  (1 shorter events, 0.0 us)
Async XLA Ops:
  0.0 2.6 %copy-start = (bf16[64,6,256]{2,0,1:T(8,128)(2,1)S(1)}, bf16[64,6,256]{2,0,1:T(8,128)(2,1)}, u32[]{:S(2)}) copy-start(bf16[64,6,256]{2,0,1:T(8,128)(2,1)} %param.14) | copy-start | bytes 589828
  2.6 0.7 copy-start.2
  3.4 0.8 copy-start.1
